TPU v7x, 512 devices: a whole 4x4x16 slice. The times are simulated.
512 devices in a mesh: ctx: 64 (over x, z), qg: 8 (over y, core).
Axes of the slice: x: 4, y: 4, z: 16, core: 2. Of those that a mesh axis runs over, the one named last changes fastest.
Arguments:
- queries: bfloat16 [32, 32, 768], P('qg'), may hold values from -9 to 9
- documents: bfloat16 [16, 32768, 768], P('qg', 'ctx'), may hold values from -2.5 to 2.5
- candidates: int32 [32, 4], replicated, may hold values from 0 to 15, all different within a row
Outputs:
- loss: float32 [], replicated
- grad_queries: bfloat16 [32, 32, 768], P('qg')
- grad_documents: bfloat16 [16, 32768, 768], P('qg', 'ctx')
Inputs may be any that keep to these rules, and one draw needn't show every extreme that they name: `candidates`: each row names 4 different documents; every document is named by some row.
All inputs are finite; a program needn't handle non-finite values.
Results may differ from a plain program's by a relative error of at most 0.006.
Values may be sent and summed in bfloat16 or wider, within the bound.
No kernel may reach another device: no remote copies, remote signals or barrier semaphores. Data moves between devices by JAX's collectives and lax.ppermute only.
A program may use at most 64 MiB of HBM per device.

v0:
```python
import jax
import jax.numpy as jnp
from jax import lax
from jax.sharding import Mesh
from jax.sharding import PartitionSpec as P

QBLOCK = 8
QG = ("qg_0", "qg_1")
CTX = ("ctx_0", "ctx_1")


sharpness_factor = 2.0
loss_scale = 1024.0
empty_stat = -1e30


def copy_for_each(x, axis):
    copies = jnp.broadcast_to(x, (lax.axis_size(axis), *x.shape))
    return lax.all_to_all(copies, axis, split_axis=0, concat_axis=0, tiled=True)


def in_order(tiles, dim):
    dims = list(tiles.shape[1:])
    dims[dim] *= tiles.shape[0]
    return jnp.moveaxis(tiles, 0, dim).reshape(dims)


def gather_axes(x, axes, dim):
    far, near = axes
    tiles = copy_for_each(copy_for_each(x, far), near)
    return in_order(tiles.swapaxes(0, 1).reshape(-1, *x.shape), dim)


def gathered_once(x, axis):
    leaves = jax.tree.leaves(x)
    turns = sorted(range(len(leaves)), key=lambda k: -leaves[k].size)
    width = (1, *leaves[turns[0]].shape)[-1]
    lines = [
        jnp.pad(leaves[k].reshape(-1), (0, -leaves[k].size % width)).reshape(-1, width)
        for k in turns
    ]
    both, at, found = (lax.all_gather(jnp.concatenate(lines), axis), 0, {})
    for k, line in zip(turns, lines):
        piece = both[:, at : at + len(line)].reshape(len(both), -1)
        found[k] = piece[:, : leaves[k].size].reshape(-1, *leaves[k].shape)
        at += len(line)
    numbers = iter(range(len(leaves)))
    return jax.tree.map(lambda _: found[next(numbers)], x)


def merged_by_axis(x, axes, combine):
    for axis in axes:
        pieces = gathered_once(x, axis)
        x = jax.tree.map(lambda part: part[0], pieces)
        for k in range(1, lax.axis_size(axis)):
            x = combine(x, jax.tree.map(lambda part: part[k], pieces))
    return x


def gather_directly(x, axis, dim):
    return in_order(copy_for_each(x, axis), dim)


def split_up(x, dim, length):
    before, after = (x.shape[:dim], x.shape[dim + 1 :])
    return jnp.moveaxis(x.reshape(*before, length, -1, *after), dim, 0)


def sent_and_summed(x, axis, dim):
    tiles = split_up(x, dim, lax.axis_size(axis))
    arrived = lax.all_to_all(tiles, axis, split_axis=0, concat_axis=0, tiled=True)
    return arrived.sum(axis=0)


def sum_by_axis(x, axes, dim):
    far, near = axes
    tiles = split_up(x, dim, lax.axis_size(far))
    nearer = sent_and_summed(tiles, near, dim + 1)
    arrived = lax.all_to_all(nearer, far, split_axis=0, concat_axis=0, tiled=True)
    return arrived.sum(axis=0)


def padded_to(lines, length):
    spare = -lines.shape[0] % length
    if not spare:
        return lines
    return jnp.concatenate([lines, jnp.zeros((spare, *lines.shape[1:]), lines.dtype)])


def sum_by_parts(x, axes):
    lines = x.reshape(-1, x.shape[-1])
    padded = padded_to(lines, lax.axis_size(axes))
    whole = gather_directly(sent_and_summed(padded, axes, 0), axes, 0)
    return lax.slice_in_dim(whole, 0, len(lines)).reshape(x.shape)


def per_device(queries, documents, candidates):
    local_docs = documents.shape[0]
    doc_len = documents.shape[1]
    query_len = queries.shape[1]
    width = queries.shape[2]
    slots = candidates.shape[1]
    everyone = gather_axes(queries, ("qg_0", "qg_1"), 0)
    total_queries = everyone.shape[0]
    all_docs = local_docs * lax.axis_size(QG)
    block = QBLOCK
    group = lax.axis_index(QG)
    doc_ids = group * local_docs + jnp.arange(local_docs, dtype=jnp.int32)
    query_iota = jnp.arange(total_queries, dtype=jnp.int32)
    counts = jnp.full((local_docs,), total_queries, jnp.int32)
    listing = jnp.broadcast_to(query_iota[:, None], (total_queries, local_docs))
    rounds = counts // block

    def take_block(selected_slot, turn):
        start = turn * block
        slot = lax.dynamic_slice_in_dim(listing[:, selected_slot], start, block)
        valid = start + jnp.arange(block, dtype=jnp.int32) < counts[selected_slot]
        rows = everyone[slot].reshape(block * query_len, width)
        candidate_logits = sharpness_factor * lax.dot_general(
            rows,
            documents[selected_slot],
            (((1,), (1,)), ((), ())),
            preferred_element_type=jnp.float32,
        )
        return (slot, valid, rows, candidate_logits)

    maxima_list = []
    totals_list = []
    for selected_slot in range(local_docs):

        def forward(turn, carry, selected_slot=selected_slot):
            top, mass = carry
            slot, valid, rows, candidate_logits = take_block(selected_slot, turn)
            peak = jnp.max(candidate_logits, axis=1)
            portion = jnp.sum(jnp.exp(candidate_logits - peak[:, None]), axis=1)
            keep = valid[:, None]
            top = top.at[slot].set(jnp.where(keep, peak.reshape(block, query_len), top[slot]))
            mass = mass.at[slot].set(jnp.where(keep, portion.reshape(block, query_len), mass[slot]))
            return (top, mass)

        start_stats = (
            jnp.full((total_queries, query_len), empty_stat, jnp.float32),
            jnp.zeros((total_queries, query_len), jnp.float32),
        )
        top, mass = lax.fori_loop(0, rounds[selected_slot], forward, start_stats)
        maxima_list.append(top)
        totals_list.append(mass)
    maxima = jnp.stack(maxima_list)
    totals = jnp.stack(totals_list)

    def combine(first, second):
        peak = jnp.maximum(first[0], second[0])
        return (peak, first[1] * jnp.exp(first[0] - peak) + second[1] * jnp.exp(second[0] - peak))

    peak, mass = merged_by_axis((maxima, totals), CTX, combine)
    seen = mass > 0.5
    log_partition = jnp.where(seen, peak + jnp.log(jnp.where(seen, mass, 1.0)), 0.0)
    partial_scores = jnp.sum(log_partition, axis=2) / sharpness_factor
    score_table = gather_directly(partial_scores, QG, 0)
    picks = (candidates[:, :, None] == jnp.arange(all_docs, dtype=jnp.int32)[None, None, :]).astype(
        jnp.float32
    )
    query_document_pair = jnp.sum(picks * jnp.transpose(score_table)[:, None, :], axis=2)
    highest = jnp.max(query_document_pair, axis=1)
    total = highest + jnp.log(jnp.sum(jnp.exp(query_document_pair - highest[:, None]), axis=1))
    loss = jnp.mean(total - query_document_pair[:, 0])
    first = (jnp.arange(slots) == 0).astype(jnp.float32)
    dz = (
        loss_scale
        / total_queries
        * (jnp.exp(query_document_pair - total[:, None]) - first[None, :])
    )
    owned = (candidates[:, :, None] == doc_ids[None, None, :]).astype(jnp.float32)
    weights = jnp.sum(dz[:, :, None] * owned, axis=1)
    grad_q = jnp.zeros((total_queries, query_len, width), jnp.float32)
    doc_grads = []
    for selected_slot in range(local_docs):

        def backward(turn, carry, selected_slot=selected_slot):
            grad_acc, grad_doc = carry
            slot, valid, rows, candidate_logits = take_block(selected_slot, turn)
            norm = log_partition[selected_slot][slot].reshape(-1)
            keep = jnp.repeat(valid, query_len)
            prob = jnp.where(keep[:, None], jnp.exp(candidate_logits - norm[:, None]), 0.0)
            row_weight = jnp.repeat(weights[slot, selected_slot], query_len)
            weighted = (row_weight[:, None] * prob).astype(jnp.bfloat16)
            grad_acc = grad_acc.at[slot].add(
                jnp.dot(
                    weighted, documents[selected_slot], preferred_element_type=jnp.float32
                ).reshape(block, query_len, width)
            )
            grad_doc = grad_doc + lax.dot_general(
                weighted, rows, (((0,), (0,)), ((), ())), preferred_element_type=jnp.float32
            )
            return (grad_acc, grad_doc)

        grad_q, grad_doc = lax.fori_loop(
            0, rounds[selected_slot], backward, (grad_q, jnp.zeros((doc_len, width), jnp.float32))
        )
        doc_grads.append(grad_doc.astype(jnp.bfloat16))
    shared = sum_by_axis(grad_q, ("qg_0", "qg_1"), 0)
    mine = sum_by_parts(shared, CTX)
    return (loss, mine.astype(jnp.bfloat16), jnp.stack(doc_grads))


def solution(mesh):
    finer = Mesh(mesh.devices.reshape(4, 16, 4, 2), ("ctx_0", "ctx_1", "qg_0", "qg_1"))
    in_specs = (P(QG, None, None), P(QG, CTX, None), P())
    out_specs = (P(), P(QG, None, None), P(QG, CTX, None))
    return jax.shard_map(
        per_device, mesh=finer, in_specs=in_specs, out_specs=out_specs, check_vma=False
    )
```

profile of v0, /device:TPU:6, one launch (start us, length us, event | category | flops | bytes accessed | tf_op | source)
XLA Modules:
  0.0 308.8 jit_solution(12166411528395523642)
XLA Ops:
  2.5 4.5 %all-to-all-start = ((bf16[4,4,32,768]{3,2,1,0:T(8,128)(2,1)}), bf16[4,4,32,768]{3,2,1,0:T(8,128)(2,1)S(1)}, u32[]{:S(2)}, u32[]{:S(2)}) async-start(bf16[4,4,32,768]{3,2,1,0:T(8,128)(2,1)} %broadcast_in_dim.137), calls=%async_computation | async-start | bytes 1572864 | tf_op jit(solution)/shard_map/all_to_all | solution.py:19
  7.0 12.3 %all-to-all-done = bf16[4,4,32,768]{3,2,1,0:T(8,128)(2,1)S(1)} async-done(((bf16[4,4,32,768]{3,2,1,0:T(8,128)(2,1)}), bf16[4,4,32,768]{3,2,1,0:T(8,128)(2,1)S(1)}, u32[]{:S(2)}, u32[]{:S(2)}) %all-to-all-start) | async-done | bytes 786464 | tf_op jit(solution)/shard_map/all_to_all | solution.py:19
  19.5 5.0 %all_to_all.35 = bf16[2,4,4,32,768]{4,3,2,1,0:T(8,128)(2,1)S(1)} all-to-all(bf16[2,4,4,32,768]{4,3,2,1,0:T(8,128)(2,1)S(1)} %broadcast_in_dim.138), channel_id=1, replica_groups=mesh['ctx_0'=4,'ctx_1'=16,'qg_0'=4,'qg_1'=2] {'qg_1'}, dimensions={0} | all-to-all | bytes 3145728 | tf_op jit(solution)/shard_map/all_to_all | solution.py:19
  24.6 16.2 %while.55 = (s32[]{:T(128)}, f32[32,32]{1,0:T(8,128)S(1)}, f32[32,32]{1,0:T(8,128)S(1)}, s32[32,2]{0,1:T(2,128)S(1)}, bf16[32,32,768]{2,1,0:T(8,128)(2,1)S(1)}, ...) while((s32[]{:T(128)}, f32[32,32]{1,0:T(8,128)S(1)}, ...), condition=%wide.region_11.12_spmd, body=%wide.region_6.11_spmd.sunk | while | flops 201851952 | bytes 3084843 | solution.py:145
  40.8 16.1 %while.54 = (s32[]{:T(128)}, f32[32,32]{1,0:T(8,128)S(1)}, f32[32,32]{1,0:T(8,128)S(1)}, s32[32,2]{0,1:T(2,128)S(1)}, bf16[32,32,768]{2,1,0:T(8,128)(2,1)S(1)}, ...) while((s32[]{:T(128)}, f32[32,32]{1,0:T(8,128)S(1)}, ...), condition=%wide.region_5.6_spmd, body=%wide.region_0.5_spmd.sunk | while | flops 201851952 | bytes 3084843 | solution.py:145
  57.2 11.9 %all-gather = f32[512,32]{0,1:T(8,128)S(1)} all-gather(f32[128,32]{0,1:T(8,128)S(1)} %pad_maximum_fusion.3), channel_id=2, replica_groups=mesh['ctx_0'=4,'ctx_1'=16,'qg_0'=4,'qg_1'=2] {'ctx_0'}, dimensions={0}, use_global_device_ids=true | all-gather | bytes 81920 | tf_op jit(solution)/shard_map/all_gather | solution.py:42
  69.4 36.8 %all-gather.1 = f32[2048,32]{0,1:T(8,128)S(1)} all-gather(f32[128,32]{0,1:T(8,128)S(1)} %pad_maximum_fusion.4), channel_id=3, replica_groups=mesh['ctx_0'=4,'ctx_1'=16,'qg_0'=4,'qg_1'=2] {'ctx_1'}, dimensions={0}, use_global_device_ids=true | all-gather | bytes 278528 | tf_op jit(solution)/shard_map/all_gather | solution.py:42
  110.5 3.3 %all-to-all-start.2 = ((f32[8,2,32]{2,1,0:T(2,128)}), f32[8,2,32]{2,1,0:T(2,128)S(1)}, u32[]{:S(2)}, u32[]{:S(2)}) async-start(f32[8,2,32]{2,1,0:T(2,128)} %broadcast_in_dim.141), calls=%async_computation.2 | async-start | bytes 16384 | tf_op jit(solution)/shard_map/all_to_all | solution.py:19
  114.0 5.0 %all-to-all-done.2 = f32[8,2,32]{2,1,0:T(2,128)S(1)} async-done(((f32[8,2,32]{2,1,0:T(2,128)}), f32[8,2,32]{2,1,0:T(2,128)S(1)}, u32[]{:S(2)}, u32[]{:S(2)}) %all-to-all-start.2) | async-done | bytes 2080 | tf_op jit(solution)/shard_map/all_to_all | solution.py:19
  121.9 44.3 %while.56 = (s32[]{:T(128)}, f32[32,32,768]{2,1,0:T(8,128)}, f32[512,768]{1,0:T(8,128)}, s32[32,2]{0,1:T(2,128)S(1)}, f32[32,2]{0,1:T(2,128)S(1)}, /*index=5*/bf...) while((s32[]{:T(128)}, f32[32,32,768]{2,1,0:T(8,128)}, ...), condition=%wide.region_20.21_spmd.clone, body=%wide.region_18.20_spmd.clone.sunk | while | flops 605619264 | bytes 10246989 | solution.py:197
  127.3 3.0 scatter_fusion
  137.4 3.1 scatter_fusion
  140.4 3.0 select_add_fusion.4
  148.8 3.1 scatter_fusion
  151.9 3.0 select_add_fusion.4
  160.2 3.1 scatter_fusion
  163.3 3.0 select_add_fusion.4
  166.3 44.3 %while.57 = (s32[]{:T(128)}, f32[32,32,768]{2,1,0:T(8,128)}, f32[512,768]{1,0:T(8,128)}, s32[32,2]{0,1:T(2,128)S(1)}, f32[32,2]{0,1:T(2,128)S(1)}, /*index=5*/bf...) while((s32[]{:T(128)}, f32[32,32,768]{2,1,0:T(8,128)}, ...), condition=%wide.region_23.24_spmd.clone, body=%wide.region_21.23_spmd.clone.sunk | while | flops 605619264 | bytes 10246989 | solution.py:197
  171.7 3.0 scatter_fusion.1
  181.7 3.1 scatter_fusion.1
  184.8 3.0 select_add_fusion.5
  193.1 3.1 scatter_fusion.1
  196.2 3.0 select_add_fusion.5
  204.6 3.1 scatter_fusion.1
  207.6 3.0 select_add_fusion.5
  210.6 2.2 copy.350
  212.8 7.2 %all_to_all.36 = f32[2,4,4,32,768]{4,3,2,1,0:T(8,128)} all-to-all(f32[2,4,4,32,768]{4,3,2,1,0:T(8,128)S(1)} %copy.350), channel_id=1, replica_groups=mesh['ctx_0'=4,'ctx_1'=16,'qg_0'=4,'qg_1'=2] {'qg_1'}, dimensions={0} | all-to-all | bytes 6291456 | tf_op jit(solution)/shard_map/all_to_all | solution.py:71
  220.0 2.3 reduce_sum.97
  222.3 23.7 %all_to_all.37 = f32[4,4,32,768]{3,2,1,0:T(8,128)S(1)} all-to-all(f32[4,4,32,768]{3,2,1,0:T(8,128)S(1)} %reduce_sum.97), channel_id=1, replica_groups=mesh['ctx_0'=4,'ctx_1'=16,'qg_0'=4,'qg_1'=2] {'qg_0'}, dimensions={0} | all-to-all | bytes 3145728 | tf_op jit(solution)/shard_map/all_to_all | solution.py:79
  246.4 35.6 %all_to_all.38 = f32[64,2,768]{2,1,0:T(2,128)S(1)} all-to-all(f32[64,2,768]{2,1,0:T(2,128)S(1)} %reshape_reshape.16), channel_id=1, replica_groups=mesh['ctx_0'=4,'ctx_1'=16,'qg_0'=4,'qg_1'=2] {'ctx_0','ctx_1'}, dimensions={0} | all-to-all | bytes 786432 | tf_op jit(solution)/shard_map/all_to_all | solution.py:71
  283.0 6.8 %all-to-all-start.6 = ((bf16[64,2,768]{2,1,0:T(2,128)(2,1)}), bf16[64,2,768]{2,1,0:T(2,128)(2,1)S(1)}, u32[]{:S(2)}, u32[]{:S(2)}) async-start(bf16[64,2,768]{2,1,0:T(2,128)(2,1)} %broadcast_in_dim.147), calls=%async_computation.6 | async-start | bytes 393216 | tf_op jit(solution)/shard_map/all_to_all | solution.py:19
  291.9 15.0 %all-to-all-done.6 = bf16[64,2,768]{2,1,0:T(2,128)(2,1)S(1)} async-done(((bf16[64,2,768]{2,1,0:T(2,128)(2,1)}), bf16[64,2,768]{2,1,0:T(2,128)(2,1)S(1)}, u32[]{:S(2)}, u32[]{:S(2)}) %all-to-all-start.6) | async-done | bytes 196640 | tf_op jit(solution)/shard_map/all_to_all | solution.py:19
  (295 shorter events, 91.4 us)
Async XLA Ops:
  2.5 16.7 %all-to-all-start = ((bf16[4,4,32,768]{3,2,1,0:T(8,128)(2,1)}), bf16[4,4,32,768]{3,2,1,0:T(8,128)(2,1)S(1)}, u32[]{:S(2)}, u32[]{:S(2)}) async-start(bf16[4,4,32,768]{3,2,1,0:T(8,128)(2,1)} %broadcast_in_dim.137), calls=%async_computation | async-start | bytes 1572864 | tf_op jit(solution)/shard_map/all_to_all | solution.py:19
  107.4 11.7 %copy-start.2 = (s32[32,4]{0,1:T(4,128)S(1)}, s32[32,4]{0,1:T(4,128)}, u32[]{:S(2)}) copy-start(s32[32,4]{0,1:T(4,128)} %param.13) | copy-start | bytes 1540
  110.5 8.6 %all-to-all-start.2 = ((f32[8,2,32]{2,1,0:T(2,128)}), f32[8,2,32]{2,1,0:T(2,128)S(1)}, u32[]{:S(2)}, u32[]{:S(2)}) async-start(f32[8,2,32]{2,1,0:T(2,128)} %broadcast_in_dim.141), calls=%async_computation.2 | async-start | bytes 16384 | tf_op jit(solution)/shard_map/all_to_all | solution.py:19
  246.2 44.3 %copy-start = (f32[512,768]{1,0:T(8,128)S(1)}, f32[512,768]{1,0:T(8,128)}, u32[]{:S(2)}) copy-start(f32[512,768]{1,0:T(8,128)} %get-tuple-element.242) | copy-start | bytes 4718596
  282.2 8.3 %copy-start.1 = (f32[512,768]{1,0:T(8,128)S(1)}, f32[512,768]{1,0:T(8,128)}, u32[]{:S(2)}) copy-start(f32[512,768]{1,0:T(8,128)} %get-tuple-element.241) | copy-start | bytes 4718596
  283.0 24.0 %all-to-all-start.6 = ((bf16[64,2,768]{2,1,0:T(2,128)(2,1)}), bf16[64,2,768]{2,1,0:T(2,128)(2,1)S(1)}, u32[]{:S(2)}, u32[]{:S(2)}) async-start(bf16[64,2,768]{2,1,0:T(2,128)(2,1)} %broadcast_in_dim.147), calls=%async_computation.6 | async-start | bytes 393216 | tf_op jit(solution)/shard_map/all_to_all | solution.py:19
where the time goes:
time: 311 us; the launch traced here: 309 us
  blocking collectives  120 us (39%)
  matrix products  58.5 us (19%)
  other arithmetic  43.7 us (14%)
  local copies, waits for them, and re-layouts  36 us (12%)
  waiting for transfers between devices  32.3 us (10%)
  starting transfers between devices  14.6 us (5%)
    all_gather x2, blocking collectives, gathered_once(): both, at, found = (lax.all_gather(jnp.concatenate(lines), axis), 0, {})  48.6 us
    all_to_all x2, blocking collectives, sent_and_summed(): lax.all_to_all(tiles, axis, split_axis=0, concat_axis=0, tiled=True)  42.9 us
    all_to_all x3, waiting for transfers between devices, copy_for_each(): return lax.all_to_all(copies, axis, split_axis=0, concat_axis=0, tiled=True)  32.3 us
    dot_general x16, matrix products, take_block(): lax.dot_general(rows, documents[selected_slot], (((1,), (1,)), ((), ())),...  25.7 us
    scatter-add x8, other arithmetic, backward(): grad_acc.at[slot]  24.5 us
    all_to_all x1, blocking collectives, sum_by_axis(): lax.all_to_all(nearer, far, split_axis=0, concat_axis=0, tiled=True)  23.7 us
    dot_general x8, matrix products, backward(): lax.dot_general(weighted, rows, (((0,), (0,)), ((), ())), preferred_eleme...  20.8 us
    all_to_all x3, starting transfers between devices, copy_for_each(): return lax.all_to_all(copies, axis, split_axis=0, concat_axis=0, tiled=True)  14.6 us
  transfers between devices with their start and end apart: 3, of which 3 were waited for; matrix products, arithmetic and copies ran while one was open for 1% of the time, Pallas kernels for 0%

commit v1 on v0

v1 whole, which is shorter than its diff:
```python
import jax
import jax.numpy as jnp
from jax import lax
from jax.sharding import Mesh
from jax.sharding import PartitionSpec as P

QG = ("y", "c")
CTX = ("x", "z")

sharpness_factor = 2.0
loss_scale = 1024.0


def copy_for_each(x, axis):
    copies = jnp.broadcast_to(x, (lax.axis_size(axis), *x.shape))
    return lax.all_to_all(copies, axis, split_axis=0, concat_axis=0, tiled=True)


def other_core(x):
    return lax.ppermute(x, "c", [(0, 1), (1, 0)])


def per_device(queries, documents, candidates):
    local_docs, doc_len, width = documents.shape
    per_group, query_len, _ = queries.shape
    slots = candidates.shape[1]
    rows_of_y = lax.axis_size("y")
    groups = lax.axis_size(QG)
    total_queries = per_group * groups
    total_rows = total_queries * query_len
    half = total_queries // 2
    core = lax.axis_index("c")

    def swap_order(t):
        pairs = t.reshape(rows_of_y, 2, per_group, *t.shape[1:])
        flip = jnp.where(core == 0, pairs, pairs[:, ::-1])
        return jnp.moveaxis(flip, 1, 0).reshape(t.shape)

    def swap_back(t):
        pairs = t.reshape(2, rows_of_y, per_group, *t.shape[1:])
        flip = jnp.where(core == 0, pairs, pairs[::-1])
        return jnp.moveaxis(flip, 0, 1).reshape(t.shape)

    own = copy_for_each(queries, "y").reshape(half * query_len, width)
    rows = jnp.concatenate([own, other_core(own)])

    logits = sharpness_factor * lax.dot_general(
        rows, documents, (((1,), (2,)), ((), ())), preferred_element_type=jnp.float32
    )
    peak = jnp.max(logits, axis=2)
    mass = jnp.sum(jnp.exp(logits - peak[:, :, None]), axis=2)
    local_lse = (peak + jnp.log(mass)).T.reshape(-1, 128)

    everywhere = copy_for_each(local_lse, CTX)
    top = jnp.max(everywhere, axis=0)
    lse = top + jnp.log(jnp.sum(jnp.exp(everywhere - top[None]), axis=0))
    lse = lse.reshape(local_docs, total_queries, query_len)

    scores = jnp.sum(lse, axis=2) / sharpness_factor
    scores = copy_for_each(swap_back(scores.T).T, QG).reshape(-1, total_queries)
    all_docs = scores.shape[0]
    picks = candidates[:, :, None] == jnp.arange(all_docs, dtype=jnp.int32)[None, None, :]
    pair = jnp.sum(jnp.where(picks, scores.T[:, None, :], 0.0), axis=2)
    highest = jnp.max(pair, axis=1)
    total = highest + jnp.log(jnp.sum(jnp.exp(pair - highest[:, None]), axis=1))
    loss = jnp.mean(total - pair[:, 0])
    first = (jnp.arange(slots) == 0).astype(jnp.float32)
    dz = loss_scale / total_queries * (jnp.exp(pair - total[:, None]) - first[None, :])
    group = lax.axis_index(QG)
    doc_ids = group * local_docs + jnp.arange(local_docs, dtype=jnp.int32)
    owned = candidates[:, :, None] == doc_ids[None, None, :]
    weights = swap_order(jnp.sum(jnp.where(owned, dz[:, :, None], 0.0), axis=1))
    row_weight = jnp.repeat(weights, query_len, axis=0)
    norm = lse.reshape(local_docs, total_rows).T

    weighted = (row_weight[:, :, None] * jnp.exp(logits - norm[:, :, None])).astype(jnp.bfloat16)
    grad_rows = lax.dot_general(
        weighted, documents, (((1, 2), (0, 1)), ((), ())), preferred_element_type=jnp.float32
    )
    grad_docs = lax.dot_general(
        weighted, rows, (((0,), (0,)), ((), ())), preferred_element_type=jnp.float32
    ).astype(jnp.bfloat16)

    mine, theirs = grad_rows[: total_rows // 2], grad_rows[total_rows // 2 :]
    chip = mine + other_core(theirs.astype(jnp.bfloat16)).astype(jnp.float32)
    tiles = chip.reshape(rows_of_y, -1, width).astype(jnp.bfloat16)
    arrived = lax.all_to_all(tiles, "y", split_axis=0, concat_axis=0, tiled=True)
    summed = jnp.sum(arrived.astype(jnp.float32), axis=0)
    tiles = summed.reshape(lax.axis_size(CTX), -1, width).astype(jnp.bfloat16)
    arrived = lax.all_to_all(tiles, CTX, split_axis=0, concat_axis=0, tiled=True)
    part = jnp.sum(arrived.astype(jnp.float32), axis=0).astype(jnp.bfloat16)
    grad_q = copy_for_each(part, CTX).reshape(queries.shape)
    return loss, grad_q, grad_docs


def solution(mesh):
    finer = Mesh(mesh.devices.reshape(4, 16, 4, 2), ("x", "z", "y", "c"))
    in_specs = (P(QG, None, None), P(QG, CTX, None), P())
    out_specs = (P(), P(QG, None, None), P(QG, CTX, None))
    return jax.shard_map(
        per_device, mesh=finer, in_specs=in_specs, out_specs=out_specs, check_vma=False
    )
```

time: 311 us -> 165 us (0.53)
  blocking collectives: 120 us -> 56 us
  matrix products: 58.5 us -> 11.7 us
  other arithmetic: 43.7 us -> 2.4 us
  local copies, waits for them, and re-layouts: 36 us -> 6.83 us
  waiting for transfers between devices: 32.3 us -> 52.6 us
  starting transfers between devices: 14.6 us -> 32.5 us
    all_gather x2 -> x0, blocking collectives: 48.6 us -> none  [gathered_once(): both, at, found = (lax.all_gather(jnp.concatenate(lines), axis), 0, {})]
    dot_general x32 -> x3, matrix products: 58.5 us -> 11.7 us  [the longest x1 5.57 us: per_device(): lax.dot_general(weighted, rows, (((0,), (0,)), ((), ())), preferred_eleme...]
    all_to_all x3 -> x2, blocking collectives: 66.6 us -> 39.5 us  [the longest x1 24.2 us: per_device(): lax.all_to_all(tiles, CTX, split_axis=0, concat_axis=0, tiled=True)]
    scatter-add x8 -> x0, other arithmetic: 24.5 us -> none  [backward(): grad_acc.at[slot]]
    gather x32 -> x0, local copies, waits for them, and re-layouts: 18.8 us -> none  [the longest x16 9.15 us: take_block(): rows = everyone[slot].reshape(block * query_len, width)]
    all_to_all x3, waiting for transfers between devices: 32.3 us -> 48.1 us  [copy_for_each(): return lax.all_to_all(copies, axis, split_axis=0, concat_axis=0, tiled=True)]
    all_to_all x3, starting transfers between devices: 14.6 us -> 28.7 us  [copy_for_each(): return lax.all_to_all(copies, axis, split_axis=0, concat_axis=0, tiled=True)]
    all_to_all x1, blocking collectives: 5 us -> 16.6 us  [copy_for_each(): return lax.all_to_all(copies, axis, split_axis=0, concat_axis=0, tiled=True)]
  transfers between devices with their start and end apart: 3 -> 5, of which waited for: 3 -> 5; matrix products, arithmetic and copies ran while one was open for 1% -> 3% of each run, Pallas kernels for 0% -> 0%
where the time goes in v1:
time: 165 us
  blocking collectives  56 us (34%)
  waiting for transfers between devices  52.6 us (32%)
  starting transfers between devices  32.5 us (20%)
  matrix products  11.7 us (7%)
  local copies, waits for them, and re-layouts  6.83 us (4%)
  between operations  2.62 us (2%)
  other arithmetic  2.4 us (1%)
    all_to_all x3, waiting for transfers between devices, copy_for_each(): return lax.all_to_all(copies, axis, split_axis=0, concat_axis=0, tiled=True)  48.1 us
    all_to_all x3, starting transfers between devices, copy_for_each(): return lax.all_to_all(copies, axis, split_axis=0, concat_axis=0, tiled=True)  28.7 us
    all_to_all x1, blocking collectives, per_device(): lax.all_to_all(tiles, CTX, split_axis=0, concat_axis=0, tiled=True)  24.2 us
    all_to_all x1, blocking collectives, copy_for_each(): return lax.all_to_all(copies, axis, split_axis=0, concat_axis=0, tiled=True)  16.6 us
    all_to_all x1, blocking collectives, per_device(): lax.all_to_all(tiles, 'y', split_axis=0, concat_axis=0, tiled=True)  15.3 us
    dot_general x1, matrix products, per_device(): lax.dot_general(weighted, rows, (((0,), (0,)), ((), ())), preferred_eleme...  5.57 us
    ppermute x2, waiting for transfers between devices, other_core(): return lax.ppermute(x, 'c', [(0, 1), (1, 0)])  4.5 us
    dot_general x1, matrix products, per_device(): lax.dot_general(weighted, documents, (((1, 2), (0, 1)), ((), ())), prefer...  4.28 us
  transfers between devices with their start and end apart: 5, of which 5 were waited for; matrix products, arithmetic and copies ran while one was open for 3% of the time, Pallas kernels for 0%

profile of v1, /device:TPU:6, one launch (start us, length us, event | category | flops | bytes accessed | tf_op | source)
XLA Modules:
  0.0 164.7 jit_solution(10033309349165718183)
XLA Ops:
  0.6 1.1 broadcast_in_dim.51
  1.8 16.6 %all_to_all.30 = bf16[4,4,32,768]{3,2,1,0:T(8,128)(2,1)S(1)} all-to-all(bf16[4,4,32,768]{3,2,1,0:T(8,128)(2,1)S(1)} %broadcast_in_dim.51), channel_id=1, replica_groups=mesh['x'=4,'z'=16,'y'=4,'c'=2] {'y'}, dimensions={0} | all-to-all | bytes 1572864 | tf_op jit(solution)/shard_map/all_to_all | solution.py:16
  18.3 1.9 %collective-permute-start = (bf16[512,768]{1,0:T(8,128)(2,1)S(1)}, bf16[512,768]{1,0:T(8,128)(2,1)S(1)}, u32[]{:S(2)}, u32[]{:S(2)}) collective-permute-start(bf16[512,768]{1,0:T(8,128)(2,1)S(1)} %bitcast.40), channel_id=1, source_target_pairs={{0,1},{1,0},{2,3},{3,2},{4,5},{5,4},{6,7},{7,6},{8,9},{9,8},{10,11... | collective-permute-start | bytes 2359304 | tf_op jit(solution)/shard_map/ppermute | solution.py:20
  20.2 2.3 %collective-permute-done = bf16[512,768]{1,0:T(8,128)(2,1)S(1)} collective-permute-done((bf16[512,768]{1,0:T(8,128)(2,1)S(1)}, bf16[512,768]{1,0:T(8,128)(2,1)S(1)}, u32[]{:S(2)}, u32[]{:S(2)}) %collective-permute-start) | collective-permute-done | bytes 786464 | tf_op jit(solution)/shard_map/ppermute | solution.py:20
  22.5 1.8 %multiply_reduce_fusion = (f32[1024,2]{0,1:T(2,128)S(1)}, f32[1024,2,512]{0,2,1:T(8,128)S(1)}) fusion(bf16[2,512,768]{2,1,0:T(8,128)(2,1)S(1)} %copy-done, bf16[512,768]{1,0:T(8,128)(2,1)S(1)} %collective-permute-done, bf16[512,768]{1,0:T(8,128)(2,1)S(1)} %bitcast.41), kind=kOutput, calls=%fused_computation.2 | convolution fusion | flops 1615853568 | bytes 7348224 | tf_op jit(solution)/shard_map/dot_general | solution.py:47
  24.4 1.9 %copy-done.1 = f32[1024,2,512]{0,2,1:T(8,128)} copy-done((f32[1024,2,512]{0,2,1:T(8,128)}, f32[1024,2,512]{0,2,1:T(8,128)S(1)}, u32[]{:S(2)}) %copy-start.1) | copy-done | bytes 4194328
  26.3 0.7 exponential_reduce_fusion
  27.0 0.8 broadcast_in_dim.52
  27.8 18.8 %all-to-all-start.1 = ((f32[64,16,128]{2,1,0:T(8,128)}), f32[64,16,128]{2,1,0:T(8,128)S(1)}, u32[]{:S(2)}, u32[]{:S(2)}) async-start(f32[64,16,128]{2,1,0:T(8,128)} %broadcast_in_dim.52), calls=%async_computation.1 | async-start | bytes 1048576 | tf_op jit(solution)/shard_map/all_to_all | solution.py:16
  46.7 32.0 %all-to-all-done.1 = f32[64,16,128]{2,1,0:T(8,128)S(1)} async-done(((f32[64,16,128]{2,1,0:T(8,128)}), f32[64,16,128]{2,1,0:T(8,128)S(1)}, u32[]{:S(2)}, u32[]{:S(2)}) %all-to-all-start.1) | async-done | bytes 524320 | tf_op jit(solution)/shard_map/all_to_all | solution.py:16
  78.7 0.1 exponential_reduce_fusion.1
  78.9 0.1 reduce_sum.89
  79.0 0.1 reshape.99
  79.1 0.1 reshape.100
  79.2 0.6 broadcast_in_dim.53
  79.8 3.3 %all-to-all-start.2 = ((f32[8,2,32]{2,1,0:T(2,128)}), f32[8,2,32]{2,1,0:T(2,128)S(1)}, u32[]{:S(2)}, u32[]{:S(2)}) async-start(f32[8,2,32]{2,1,0:T(2,128)} %broadcast_in_dim.53), calls=%async_computation.2 | async-start | bytes 16384 | tf_op jit(solution)/shard_map/all_to_all | solution.py:16
  83.2 5.2 %all-to-all-done.2 = f32[8,2,32]{2,1,0:T(2,128)S(1)} async-done(((f32[8,2,32]{2,1,0:T(2,128)}), f32[8,2,32]{2,1,0:T(2,128)S(1)}, u32[]{:S(2)}, u32[]{:S(2)}) %all-to-all-start.2) | async-done | bytes 2080 | tf_op jit(solution)/shard_map/all_to_all | solution.py:16
  88.5 0.6 fusion.3
  89.1 0.1 select_reduce_fusion.1
  89.6 4.3 %convolution_bitcast_fusion = f32[1024,768]{1,0:T(8,128)S(1)} fusion(bf16[2,512,768]{2,1,0:T(8,128)(2,1)S(1)} %copy-done, f32[1024,2,512]{0,2,1:T(8,128)} %copy-done.1, f32[1024,2]{0,1:T(2,128)S(1)} %bitcast.44, f32[1024,2]{0,1:T(2,128)S(1)} %mul.38), kind=kOutput, calls=%fused_computation.3 | convolution fusion | flops 1614807040 | bytes 8929280 | tf_op jit(solution)/shard_map/dot_general | solution.py:77
  94.0 1.9 %collective-permute-start.1 = (bf16[512,768]{1,0:T(8,128)(2,1)S(1)}, bf16[512,768]{1,0:T(8,128)(2,1)S(1)}, u32[]{:S(2)}, u32[]{:S(2)}) collective-permute-start(bf16[512,768]{1,0:T(8,128)(2,1)S(1)} %slice.20), channel_id=1, source_target_pairs={{0,1},{1,0},{2,3},{3,2},{4,5},{5,4},{6,7},{7,6},{8,9},{9,8},{10,11... | collective-permute-start | bytes 2359304 | tf_op jit(solution)/shard_map/ppermute | solution.py:20
  95.9 2.3 %collective-permute-done.1 = bf16[512,768]{1,0:T(8,128)(2,1)S(1)} collective-permute-done((bf16[512,768]{1,0:T(8,128)(2,1)S(1)}, bf16[512,768]{1,0:T(8,128)(2,1)S(1)}, u32[]{:S(2)}, u32[]{:S(2)}) %collective-permute-start.1) | collective-permute-done | bytes 786464 | tf_op jit(solution)/shard_map/ppermute | solution.py:20
  98.2 0.2 fusion
  98.4 15.3 %all_to_all.31 = bf16[4,128,768]{2,1,0:T(8,128)(2,1)S(1)} all-to-all(bf16[4,128,768]{2,1,0:T(8,128)(2,1)S(1)} %bitcast.39), channel_id=1, replica_groups=mesh['x'=4,'z'=16,'y'=4,'c'=2] {'y'}, dimensions={0} | all-to-all | bytes 1572864 | tf_op jit(solution)/shard_map/all_to_all | solution.py:87
  113.7 0.1 reduce_sum.94
  113.9 24.2 %all_to_all.32 = bf16[64,2,768]{2,1,0:T(2,128)(2,1)S(1)} all-to-all(bf16[64,2,768]{2,1,0:T(2,128)(2,1)S(1)} %convert_element_type.35), channel_id=1, replica_groups=mesh['x'=4,'z'=16,'y'=4,'c'=2] {'x','z'}, dimensions={0} | all-to-all | bytes 393216 | tf_op jit(solution)/shard_map/all_to_all | solution.py:90
  138.1 0.2 reduce_sum.95
  138.3 0.8 broadcast_in_dim.59
  139.1 6.6 %all-to-all-start.5 = ((bf16[64,2,768]{2,1,0:T(2,128)(2,1)}), bf16[64,2,768]{2,1,0:T(2,128)(2,1)S(1)}, u32[]{:S(2)}, u32[]{:S(2)}) async-start(bf16[64,2,768]{2,1,0:T(2,128)(2,1)} %broadcast_in_dim.59), calls=%async_computation.5 | async-start | bytes 393216 | tf_op jit(solution)/shard_map/all_to_all | solution.py:16
  146.3 5.6 %convolution_convert_fusion = bf16[2,512,768]{2,1,0:T(8,128)(2,1)} fusion(bf16[512,768]{1,0:T(8,128)(2,1)} %copy-done.3, bf16[512,768]{1,0:T(8,128)(2,1)S(1)} %bitcast.42, f32[1024,2,512]{0,2,1:T(8,128)} %copy-done.1, f32[1024,2]{0,1:T(2,128)S(1)} %bitcast.45, f32[1024,2]{0,1:T(2,128)S(1)} %mul.38), kind=kOutput, calls=%fused_computation.4 | convolution fusion | flops 1618739200 | bytes 7356416 | tf_op jit(solution)/shard_map/dot_general | solution.py:80
  151.9 10.9 %all-to-all-done.5 = bf16[64,2,768]{2,1,0:T(2,128)(2,1)S(1)} async-done(((bf16[64,2,768]{2,1,0:T(2,128)(2,1)}), bf16[64,2,768]{2,1,0:T(2,128)(2,1)S(1)}, u32[]{:S(2)}, u32[]{:S(2)}) %all-to-all-start.5) | async-done | bytes 196640 | tf_op jit(solution)/shard_map/all_to_all | solution.py:16
  162.8 0.8 reshape.104
  (31 shorter events, 0.9 us)
Async XLA Ops:
  0.6 21.9 %copy-start = (bf16[2,512,768]{2,1,0:T(8,128)(2,1)S(1)}, bf16[2,512,768]{2,1,0:T(8,128)(2,1)}, u32[]{:S(2)}) copy-start(bf16[2,512,768]{2,1,0:T(8,128)(2,1)} %param.4) | copy-start | bytes 4718596
  18.3 4.2 %collective-permute-start = (bf16[512,768]{1,0:T(8,128)(2,1)S(1)}, bf16[512,768]{1,0:T(8,128)(2,1)S(1)}, u32[]{:S(2)}, u32[]{:S(2)}) collective-permute-start(bf16[512,768]{1,0:T(8,128)(2,1)S(1)} %bitcast.40), channel_id=1, source_target_pairs={{0,1},{1,0},{2,3},{3,2},{4,5},{5,4},{6,7},{7,6},{8,9},{9,8},{10,11... | collective-permute-start | bytes 2359304 | tf_op jit(solution)/shard_map/ppermute | solution.py:20
  22.5 1.8 %copy-start.3 = (bf16[512,768]{1,0:T(8,128)(2,1)}, bf16[512,768]{1,0:T(8,128)(2,1)S(1)}, u32[]{:S(2)}) copy-start(bf16[512,768]{1,0:T(8,128)(2,1)S(1)} %collective-permute-done) | copy-start | bytes 2359300
  24.3 1.9 %copy-start.1 = (f32[1024,2,512]{0,2,1:T(8,128)}, f32[1024,2,512]{0,2,1:T(8,128)S(1)}, u32[]{:S(2)}) copy-start(f32[1024,2,512]{0,2,1:T(8,128)S(1)} %get-tuple-element.6) | copy-start | bytes 12582916
  26.3 62.1 %copy-start.2 = (s32[32,4]{0,1:T(4,128)S(1)}, s32[32,4]{0,1:T(4,128)}, u32[]{:S(2)}) copy-start(s32[32,4]{0,1:T(4,128)} %param.5) | copy-start | bytes 1540
  27.8 50.8 %all-to-all-start.1 = ((f32[64,16,128]{2,1,0:T(8,128)}), f32[64,16,128]{2,1,0:T(8,128)S(1)}, u32[]{:S(2)}, u32[]{:S(2)}) async-start(f32[64,16,128]{2,1,0:T(8,128)} %broadcast_in_dim.52), calls=%async_computation.1 | async-start | bytes 1048576 | tf_op jit(solution)/shard_map/all_to_all | solution.py:16
  79.8 8.6 %all-to-all-start.2 = ((f32[8,2,32]{2,1,0:T(2,128)}), f32[8,2,32]{2,1,0:T(2,128)S(1)}, u32[]{:S(2)}, u32[]{:S(2)}) async-start(f32[8,2,32]{2,1,0:T(2,128)} %broadcast_in_dim.53), calls=%async_computation.2 | async-start | bytes 16384 | tf_op jit(solution)/shard_map/all_to_all | solution.py:16
  94.0 4.2 %collective-permute-start.1 = (bf16[512,768]{1,0:T(8,128)(2,1)S(1)}, bf16[512,768]{1,0:T(8,128)(2,1)S(1)}, u32[]{:S(2)}, u32[]{:S(2)}) collective-permute-start(bf16[512,768]{1,0:T(8,128)(2,1)S(1)} %slice.20), channel_id=1, source_target_pairs={{0,1},{1,0},{2,3},{3,2},{4,5},{5,4},{6,7},{7,6},{8,9},{9,8},{10,11... | collective-permute-start | bytes 2359304 | tf_op jit(solution)/shard_map/ppermute | solution.py:20
  139.1 23.7 %all-to-all-start.5 = ((bf16[64,2,768]{2,1,0:T(2,128)(2,1)}), bf16[64,2,768]{2,1,0:T(2,128)(2,1)S(1)}, u32[]{:S(2)}, u32[]{:S(2)}) async-start(bf16[64,2,768]{2,1,0:T(2,128)(2,1)} %broadcast_in_dim.59), calls=%async_computation.5 | async-start | bytes 393216 | tf_op jit(solution)/shard_map/all_to_all | solution.py:16

commit v2 on v1

v2 whole, which is shorter than its diff:
```python
import jax
import jax.numpy as jnp
from jax import lax
from jax.sharding import Mesh
from jax.sharding import PartitionSpec as P

QG = ("y", "c")
CTX = ("x", "z")

sharpness_factor = 2.0
loss_scale = 1024.0


def copy_for_each(x, axis):
    copies = jnp.broadcast_to(x, (lax.axis_size(axis), *x.shape))
    return lax.all_to_all(copies, axis, split_axis=0, concat_axis=0, tiled=True)


def other_core(x):
    return lax.ppermute(x, "c", [(0, 1), (1, 0)])


def log_of_sum(x):
    top = jnp.max(x, axis=0)
    return top + jnp.log(jnp.sum(jnp.exp(x - top[None]), axis=0))


def sent_and_summed(x, axis):
    tiles = x.astype(jnp.bfloat16).reshape(lax.axis_size(axis), -1, x.shape[-1])
    arrived = lax.all_to_all(tiles, axis, split_axis=0, concat_axis=0, tiled=True)
    return jnp.sum(arrived.astype(jnp.float32), axis=0)


def per_device(queries, documents, candidates):
    local_docs, doc_len, width = documents.shape
    per_group, query_len, _ = queries.shape
    slots = candidates.shape[1]
    rows_of_y = lax.axis_size("y")
    groups = lax.axis_size(QG)
    total_queries = per_group * groups
    half_rows = total_queries * query_len // 2
    core = lax.axis_index("c")

    def swap_order(t):
        pairs = t.reshape(rows_of_y, 2, per_group, *t.shape[1:])
        flip = jnp.where(core == 0, pairs, pairs[:, ::-1])
        return jnp.moveaxis(flip, 1, 0).reshape(t.shape)

    def swap_back(t):
        pairs = t.reshape(2, rows_of_y, per_group, *t.shape[1:])
        flip = jnp.where(core == 0, pairs, pairs[::-1])
        return jnp.moveaxis(flip, 0, 1).reshape(t.shape)

    own = copy_for_each(queries, "y").reshape(half_rows, width)
    halves = [own, other_core(own)]

    logits, local_lse = [], []
    for rows in halves:
        part = sharpness_factor * lax.dot_general(
            rows, documents, (((1,), (2,)), ((), ())), preferred_element_type=jnp.float32
        )
        peak = jnp.max(part, axis=2)
        mass = jnp.sum(jnp.exp(part - peak[:, :, None]), axis=2)
        logits.append(part)
        local_lse.append(peak + jnp.log(mass))

    lse = jnp.concatenate(local_lse).T.reshape(-1, 128)
    lse = log_of_sum(copy_for_each(lse, "x"))
    lse = log_of_sum(copy_for_each(lse, "z"))
    lse, candidates = lax.optimization_barrier((lse, candidates))
    lse = lse.reshape(local_docs, total_queries, query_len)

    scores = jnp.sum(lse, axis=2) / sharpness_factor
    scores = copy_for_each(swap_back(scores.T).T, QG).reshape(-1, total_queries)
    all_docs = scores.shape[0]
    picks = candidates[:, :, None] == jnp.arange(all_docs, dtype=jnp.int32)[None, None, :]
    pair = jnp.sum(jnp.where(picks, scores.T[:, None, :], 0.0), axis=2)
    highest = jnp.max(pair, axis=1)
    total = highest + jnp.log(jnp.sum(jnp.exp(pair - highest[:, None]), axis=1))
    loss = jnp.mean(total - pair[:, 0])
    first = (jnp.arange(slots) == 0).astype(jnp.float32)
    dz = loss_scale / total_queries * (jnp.exp(pair - total[:, None]) - first[None, :])
    group = lax.axis_index(QG)
    doc_ids = group * local_docs + jnp.arange(local_docs, dtype=jnp.int32)
    owned = candidates[:, :, None] == doc_ids[None, None, :]
    weights = swap_order(jnp.sum(jnp.where(owned, dz[:, :, None], 0.0), axis=1))
    row_weight = jnp.repeat(weights, query_len, axis=0)
    norm = lse.reshape(local_docs, -1).T

    def weighted_half(k):
        at = slice(k * half_rows, (k + 1) * half_rows)
        prob = jnp.exp(logits[k] - norm[at, :, None])
        return (row_weight[at, :, None] * prob).astype(jnp.bfloat16)

    def grad_of_rows(weighted):
        return lax.dot_general(
            weighted, documents, (((1, 2), (0, 1)), ((), ())), preferred_element_type=jnp.float32
        )

    weighted = [weighted_half(0), weighted_half(1)]
    received = other_core(grad_of_rows(weighted[1]).astype(jnp.bfloat16))
    chip = grad_of_rows(weighted[0]) + received.astype(jnp.float32)
    summed = sent_and_summed(chip, ("y", "x"))
    part = sent_and_summed(summed, "z").astype(jnp.bfloat16)
    grad_q = copy_for_each(part, CTX).reshape(queries.shape)
    grad_docs = sum(
        lax.dot_general(
            weighted[k], halves[k], (((0,), (0,)), ((), ())), preferred_element_type=jnp.float32
        )
        for k in range(2)
    ).astype(jnp.bfloat16)
    return loss, grad_q, grad_docs


def solution(mesh):
    finer = Mesh(mesh.devices.reshape(4, 16, 4, 2), ("x", "z", "y", "c"))
    in_specs = (P(QG, None, None), P(QG, CTX, None), P())
    out_specs = (P(), P(QG, None, None), P(QG, CTX, None))
    return jax.shard_map(
        per_device, mesh=finer, in_specs=in_specs, out_specs=out_specs, check_vma=False
    )
```

time: 165 us -> 146 us (0.88)
  blocking collectives: 56 us -> 41.6 us
  waiting for transfers between devices: 52.6 us -> 44.5 us
  matrix products: 11.7 us -> 13.7 us
    all_to_all x2 -> x1, blocking collectives: 39.5 us -> 17.1 us  [sent_and_summed(): lax.all_to_all(tiles, axis, split_axis=0, concat_axis=0, tiled=True)]
    all_to_all x3, waiting for transfers between devices: 48.1 us -> 30.1 us  [copy_for_each(): return lax.all_to_all(copies, axis, split_axis=0, concat_axis=0, tiled=True)]
    all_to_all x0 -> x1, waiting for transfers between devices: none -> 12.1 us  [sent_and_summed(): lax.all_to_all(tiles, axis, split_axis=0, concat_axis=0, tiled=True)]
    all_to_all x1 -> x2, blocking collectives: 16.6 us -> 24.5 us  [copy_for_each(): return lax.all_to_all(copies, axis, split_axis=0, concat_axis=0, tiled=True)]
    all_to_all x0 -> x1, starting transfers between devices: none -> 3.79 us  [sent_and_summed(): lax.all_to_all(tiles, axis, split_axis=0, concat_axis=0, tiled=True)]
    all_to_all x3, starting transfers between devices: 28.7 us -> 25.6 us  [copy_for_each(): return lax.all_to_all(copies, axis, split_axis=0, concat_axis=0, tiled=True)]
    ppermute x2, waiting for transfers between devices: 4.5 us -> 2.35 us  [other_core(): return lax.ppermute(x, 'c', [(0, 1), (1, 0)])]
    dot_general x2 -> x4, matrix products: 9.86 us -> 11.7 us  [the longest x2 6.5 us: grad_of_rows(): lax.dot_general(weighted, documents, (((1, 2), (0, 1)), ((), ())), prefer...]
  transfers between devices with their start and end apart: 5 -> 6, of which waited for: 5 -> 5; matrix products, arithmetic and copies ran while one was open for 3% -> 5% of each run, Pallas kernels for 0% -> 0%
where the time goes in v2:
time: 146 us; the launch traced here: 145 us
  waiting for transfers between devices  44.5 us (30%)
  blocking collectives  41.6 us (28%)
  starting transfers between devices  33.2 us (23%)
  matrix products  13.7 us (9%)
  local copies, waits for them, and re-layouts  7.78 us (5%)
  between operations  2.7 us (2%)
  other arithmetic  1.97 us (1%)
    all_to_all x3, waiting for transfers between devices, copy_for_each(): return lax.all_to_all(copies, axis, split_axis=0, concat_axis=0, tiled=True)  30.1 us
    all_to_all x3, starting transfers between devices, copy_for_each(): return lax.all_to_all(copies, axis, split_axis=0, concat_axis=0, tiled=True)  25.6 us
    all_to_all x2, blocking collectives, copy_for_each(): return lax.all_to_all(copies, axis, split_axis=0, concat_axis=0, tiled=True)  24.5 us
    all_to_all x1, blocking collectives, sent_and_summed(): lax.all_to_all(tiles, axis, split_axis=0, concat_axis=0, tiled=True)  17.1 us
    all_to_all x1, waiting for transfers between devices, sent_and_summed(): lax.all_to_all(tiles, axis, split_axis=0, concat_axis=0, tiled=True)  12.1 us
    dot_general x2, matrix products, grad_of_rows(): lax.dot_general(weighted, documents, (((1, 2), (0, 1)), ((), ())), prefer...  6.5 us
    dot_general x2, matrix products, per_device(): lax.dot_general(weighted[k], halves[k], (((0,), (0,)), ((), ())), preferr...  5.16 us
    ppermute x2, starting transfers between devices, other_core(): return lax.ppermute(x, 'c', [(0, 1), (1, 0)])  3.82 us
  transfers between devices with their start and end apart: 6, of which 5 were waited for; matrix products, arithmetic and copies ran while one was open for 5% of the time, Pallas kernels for 0%

profile of v2, /device:TPU:6, one launch (start us, length us, event | category | flops | bytes accessed | tf_op | source)
XLA Modules:
  0.0 145.4 jit_solution(14758233018007453029)
XLA Ops:
  0.6 1.1 broadcast_in_dim.38
  1.8 16.6 %all_to_all.35 = bf16[4,4,32,768]{3,2,1,0:T(8,128)(2,1)S(1)} all-to-all(bf16[4,4,32,768]{3,2,1,0:T(8,128)(2,1)S(1)} %broadcast_in_dim.38), channel_id=1, replica_groups=mesh['x'=4,'z'=16,'y'=4,'c'=2] {'y'}, dimensions={0} | all-to-all | bytes 1572864 | tf_op jit(solution)/shard_map/all_to_all | solution.py:16
  18.3 1.9 %collective-permute-start = (bf16[512,768]{1,0:T(8,128)(2,1)S(1)}, bf16[512,768]{1,0:T(8,128)(2,1)S(1)}, u32[]{:S(2)}, u32[]{:S(2)}) collective-permute-start(bf16[512,768]{1,0:T(8,128)(2,1)S(1)} %bitcast.54), channel_id=1, source_target_pairs={{0,1},{1,0},{2,3},{3,2},{4,5},{5,4},{6,7},{7,6},{8,9},{9,8},{10,11... | collective-permute-start | bytes 2359304 | tf_op jit(solution)/shard_map/ppermute | solution.py:20
  20.2 1.0 multiply_reduce_fusion.1
  21.3 0.4 exponential_reduce_fusion.1
  21.6 1.0 copy-done.3
  22.6 1.0 multiply_reduce_fusion
  23.7 1.3 copy-done.1
  25.0 0.4 exponential_reduce_fusion
  25.4 8.0 %all_to_all.36 = f32[4,16,128]{2,1,0:T(8,128)S(1)} all-to-all(f32[4,16,128]{2,1,0:T(8,128)S(1)} %broadcast_in_dim.62), channel_id=1, replica_groups=mesh['x'=4,'z'=16,'y'=4,'c'=2] {'x'}, dimensions={0} | all-to-all | bytes 65536 | tf_op jit(solution)/shard_map/all_to_all | solution.py:16
  33.4 0.7 broadcast_in_dim.63
  34.1 15.2 %all-to-all-start.2 = ((f32[16,16,128]{2,1,0:T(8,128)}), f32[16,16,128]{2,1,0:T(8,128)S(1)}, u32[]{:S(2)}, u32[]{:S(2)}) async-start(f32[16,16,128]{2,1,0:T(8,128)} %broadcast_in_dim.63), calls=%async_computation.2 | async-start | bytes 262144 | tf_op jit(solution)/shard_map/all_to_all | solution.py:16
  49.3 13.9 %all-to-all-done.2 = f32[16,16,128]{2,1,0:T(8,128)S(1)} async-done(((f32[16,16,128]{2,1,0:T(8,128)}), f32[16,16,128]{2,1,0:T(8,128)S(1)}, u32[]{:S(2)}, u32[]{:S(2)}) %all-to-all-start.2) | async-done | bytes 131104 | tf_op jit(solution)/shard_map/all_to_all | solution.py:16
  63.7 0.6 broadcast_in_dim.64
  64.3 3.3 %all-to-all-start.3 = ((f32[8,2,32]{2,1,0:T(2,128)}), f32[8,2,32]{2,1,0:T(2,128)S(1)}, u32[]{:S(2)}, u32[]{:S(2)}) async-start(f32[8,2,32]{2,1,0:T(2,128)} %broadcast_in_dim.64), calls=%async_computation.3 | async-start | bytes 16384 | tf_op jit(solution)/shard_map/all_to_all | solution.py:16
  67.7 5.2 %all-to-all-done.3 = f32[8,2,32]{2,1,0:T(2,128)S(1)} async-done(((f32[8,2,32]{2,1,0:T(2,128)}), f32[8,2,32]{2,1,0:T(2,128)S(1)}, u32[]{:S(2)}, u32[]{:S(2)}) %all-to-all-start.3) | async-done | bytes 2080 | tf_op jit(solution)/shard_map/all_to_all | solution.py:16
  73.0 0.6 fusion.6
  74.2 3.6 %bitcast_convert_fusion = bf16[512,768]{1,0:T(8,128)(2,1)} fusion(bf16[2,512,768]{2,1,0:T(8,128)(2,1)S(1)} %copy-done, f32[512,2,512]{0,2,1:T(8,128)} %copy-done.1, f32[512,2]{0,1:T(2,128)S(1)} %get-tuple-element.12, f32[512,2]{0,1:T(2,128)S(1)} %mul.51), kind=kOutput, calls=%fused_computation.7 | convolution fusion | flops 807796736 | bytes 4464640 | tf_op jit(solution)/shard_map/dot_general | solution.py:96
  77.8 1.9 %collective-permute-start.1 = (bf16[512,768]{1,0:T(8,128)(2,1)}, bf16[512,768]{1,0:T(8,128)(2,1)}, u32[]{:S(2)}, u32[]{:S(2)}) collective-permute-start(bf16[512,768]{1,0:T(8,128)(2,1)} %bitcast_convert_fusion), channel_id=1, source_target_pairs={{0,1},{1,0},{2,3},{3,2},{4,5},{5,4},{6,7},{7,6},{8,9},{9,8},{10,11... | collective-permute-start | bytes 2359304 | tf_op jit(solution)/shard_map/ppermute | solution.py:20
  79.9 2.4 %collective-permute-done.1 = bf16[512,768]{1,0:T(8,128)(2,1)} collective-permute-done((bf16[512,768]{1,0:T(8,128)(2,1)}, bf16[512,768]{1,0:T(8,128)(2,1)}, u32[]{:S(2)}, u32[]{:S(2)}) %collective-permute-start.1) | collective-permute-done | bytes 786464 | tf_op jit(solution)/shard_map/ppermute | solution.py:20
  82.3 2.9 %fusion = bf16[512,768]{1,0:T(8,128)(2,1)S(1)} fusion(bf16[512,768]{1,0:T(8,128)(2,1)} %collective-permute-done.1, bf16[2,512,768]{2,1,0:T(8,128)(2,1)S(1)} %copy-done, f32[512,2,512]{0,2,1:T(8,128)} %copy-done.3, f32[512,2]{0,1:T(2,128)S(1)} %get-tuple-element.11, f32[512,2]{0,1:T(2,128)S(1)} %mul.48), kind=kOutput, calls=%fused_computation.9 | convolution fusion | flops 808583168 | bytes 5251072 | tf_op jit(solution)/shard_map/dot_general | solution.py:96
  85.2 17.1 %all_to_all.37 = bf16[16,32,768]{2,1,0:T(8,128)(2,1)S(1)} all-to-all(bf16[16,32,768]{2,1,0:T(8,128)(2,1)S(1)} %bitcast.57), channel_id=1, replica_groups=mesh['x'=4,'z'=16,'y'=4,'c'=2] {'y','x'}, dimensions={0} | all-to-all | bytes 1572864 | tf_op jit(solution)/shard_map/all_to_all | solution.py:30
  102.2 0.1 reduce_sum.114
  102.3 0.6 reshape.110
  103.0 3.8 %all-to-all-start.5 = ((bf16[16,2,768]{2,1,0:T(2,128)(2,1)}), bf16[16,2,768]{2,1,0:T(2,128)(2,1)S(1)}, u32[]{:S(2)}, u32[]{:S(2)}) async-start(bf16[16,2,768]{2,1,0:T(2,128)(2,1)} %reshape.110), calls=%async_computation.5 | async-start | bytes 98304 | tf_op jit(solution)/shard_map/all_to_all | solution.py:30
  107.4 12.1 %all-to-all-done.5 = bf16[16,2,768]{2,1,0:T(2,128)(2,1)S(1)} async-done(((bf16[16,2,768]{2,1,0:T(2,128)(2,1)}), bf16[16,2,768]{2,1,0:T(2,128)(2,1)S(1)}, u32[]{:S(2)}, u32[]{:S(2)}) %all-to-all-start.5) | async-done | bytes 49184 | tf_op jit(solution)/shard_map/all_to_all | solution.py:30
  119.6 0.8 broadcast_in_dim.71
  120.3 7.0 %all-to-all-start.6 = ((bf16[64,2,768]{2,1,0:T(2,128)(2,1)}), bf16[64,2,768]{2,1,0:T(2,128)(2,1)S(1)}, u32[]{:S(2)}, u32[]{:S(2)}) async-start(bf16[64,2,768]{2,1,0:T(2,128)(2,1)} %broadcast_in_dim.71), calls=%async_computation.6 | async-start | bytes 393216 | tf_op jit(solution)/shard_map/all_to_all | solution.py:16
  127.4 2.8 %fusion.4 = f32[2,512,768]{2,1,0:T(8,128)S(1)} fusion(bf16[512,768,1]{1,0,2:T(8,128)(2,1)S(1)} %bitcast.56, f32[512,2,512]{0,2,1:T(8,128)} %copy-done.3, f32[512,2]{0,1:T(2,128)S(1)} %get-tuple-element.11, f32[512,2]{0,1:T(2,128)S(1)} %mul.48), kind=kOutput, calls=%fused_computation.17 | convolution fusion | flops 807403520 | bytes 6037504 | tf_op jit(solution)/shard_map/dot_general | solution.py:107
  130.3 2.3 %add_convert_fusion = bf16[2,512,768]{2,1,0:T(8,128)(2,1)} fusion(f32[2,512,768]{2,1,0:T(8,128)S(1)} %fusion.4, bf16[512,768]{1,0:T(8,128)(2,1)S(1)} %copy-done.5, f32[512,2,512]{0,2,1:T(8,128)S(1)} %copy-done.2, f32[512,2]{0,1:T(2,128)S(1)} %get-tuple-element.12, f32[512,2]{0,1:T(2,128)S(1)} %mul.51), kind=kOutput, calls=%fused_computation | convolution fusion | flops 808976384 | bytes 7610368 | tf_op jit(solution)/shard_map/dot_general | solution.py:107
  132.6 10.9 %all-to-all-done.6 = bf16[64,2,768]{2,1,0:T(2,128)(2,1)S(1)} async-done(((bf16[64,2,768]{2,1,0:T(2,128)(2,1)}), bf16[64,2,768]{2,1,0:T(2,128)(2,1)S(1)}, u32[]{:S(2)}, u32[]{:S(2)}) %all-to-all-start.6) | async-done | bytes 196640 | tf_op jit(solution)/shard_map/all_to_all | solution.py:16
  143.5 0.8 reshape.111
  (50 shorter events, 1.5 us)
Async XLA Ops:
  0.6 19.6 %copy-start = (bf16[2,512,768]{2,1,0:T(8,128)(2,1)S(1)}, bf16[2,512,768]{2,1,0:T(8,128)(2,1)}, u32[]{:S(2)}) copy-start(bf16[2,512,768]{2,1,0:T(8,128)(2,1)} %param.4) | copy-start | bytes 4718596
  18.3 4.3 %collective-permute-start = (bf16[512,768]{1,0:T(8,128)(2,1)S(1)}, bf16[512,768]{1,0:T(8,128)(2,1)S(1)}, u32[]{:S(2)}, u32[]{:S(2)}) collective-permute-start(bf16[512,768]{1,0:T(8,128)(2,1)S(1)} %bitcast.54), channel_id=1, source_target_pairs={{0,1},{1,0},{2,3},{3,2},{4,5},{5,4},{6,7},{7,6},{8,9},{9,8},{10,11... | collective-permute-start | bytes 2359304 | tf_op jit(solution)/shard_map/ppermute | solution.py:20
  21.3 1.4 copy-start.3
  22.6 1.0 copy-start.4
  23.7 1.3 copy-start.1
  23.7 49.2 %copy-start.6 = (s32[32,4]{0,1:T(4,128)S(1)}, s32[32,4]{0,1:T(4,128)}, u32[]{:S(2)}) copy-start(s32[32,4]{0,1:T(4,128)} %param.5) | copy-start | bytes 1540
  34.1 29.2 %all-to-all-start.2 = ((f32[16,16,128]{2,1,0:T(8,128)}), f32[16,16,128]{2,1,0:T(8,128)S(1)}, u32[]{:S(2)}, u32[]{:S(2)}) async-start(f32[16,16,128]{2,1,0:T(8,128)} %broadcast_in_dim.63), calls=%async_computation.2 | async-start | bytes 262144 | tf_op jit(solution)/shard_map/all_to_all | solution.py:16
  64.3 8.6 %all-to-all-start.3 = ((f32[8,2,32]{2,1,0:T(2,128)}), f32[8,2,32]{2,1,0:T(2,128)S(1)}, u32[]{:S(2)}, u32[]{:S(2)}) async-start(f32[8,2,32]{2,1,0:T(2,128)} %broadcast_in_dim.64), calls=%async_computation.3 | async-start | bytes 16384 | tf_op jit(solution)/shard_map/all_to_all | solution.py:16
  77.8 4.5 %collective-permute-start.1 = (bf16[512,768]{1,0:T(8,128)(2,1)}, bf16[512,768]{1,0:T(8,128)(2,1)}, u32[]{:S(2)}, u32[]{:S(2)}) collective-permute-start(bf16[512,768]{1,0:T(8,128)(2,1)} %bitcast_convert_fusion), channel_id=1, source_target_pairs={{0,1},{1,0},{2,3},{3,2},{4,5},{5,4},{6,7},{7,6},{8,9},{9,8},{10,11... | collective-permute-start | bytes 2359304 | tf_op jit(solution)/shard_map/ppermute | solution.py:20
  103.0 16.5 %all-to-all-start.5 = ((bf16[16,2,768]{2,1,0:T(2,128)(2,1)}), bf16[16,2,768]{2,1,0:T(2,128)(2,1)S(1)}, u32[]{:S(2)}, u32[]{:S(2)}) async-start(bf16[16,2,768]{2,1,0:T(2,128)(2,1)} %reshape.110), calls=%async_computation.5 | async-start | bytes 98304 | tf_op jit(solution)/shard_map/all_to_all | solution.py:30
  120.3 23.2 %all-to-all-start.6 = ((bf16[64,2,768]{2,1,0:T(2,128)(2,1)}), bf16[64,2,768]{2,1,0:T(2,128)(2,1)S(1)}, u32[]{:S(2)}, u32[]{:S(2)}) async-start(bf16[64,2,768]{2,1,0:T(2,128)(2,1)} %broadcast_in_dim.71), calls=%async_computation.6 | async-start | bytes 393216 | tf_op jit(solution)/shard_map/all_to_all | solution.py:16
  127.4 2.9 %copy-start.2 = (f32[512,2,512]{0,2,1:T(8,128)S(1)}, f32[512,2,512]{0,2,1:T(8,128)}, u32[]{:S(2)}) copy-start(f32[512,2,512]{0,2,1:T(8,128)} %copy-done.1) | copy-start | bytes 6291460
  127.4 2.9 %copy-start.5 = (bf16[512,768]{1,0:T(8,128)(2,1)S(1)}, bf16[512,768]{1,0:T(8,128)(2,1)}, u32[]{:S(2)}) copy-start(bf16[512,768]{1,0:T(8,128)(2,1)} %copy-done.4) | copy-start | bytes 2359300

commit v3 on v2

v3 whole, which is shorter than its diff:
```python
import jax
import jax.numpy as jnp
from jax import lax
from jax.sharding import Mesh
from jax.sharding import PartitionSpec as P

QG = ("y", "c")
CTX = ("x", "h", "l")

sharpness_factor = 2.0
loss_scale = 1024.0


def copy_for_each(x, axis):
    copies = jnp.broadcast_to(x, (lax.axis_size(axis), *x.shape))
    return lax.all_to_all(copies, axis, split_axis=0, concat_axis=0, tiled=True)


def other_core(x):
    return lax.ppermute(x, "c", [(0, 1), (1, 0)])


def log_of_sum(x):
    top = jnp.max(x, axis=0)
    return top + jnp.log(jnp.sum(jnp.exp(x - top[None]), axis=0))


def sent_and_summed(x, axis):
    tiles = x.astype(jnp.bfloat16).reshape(lax.axis_size(axis), -1, x.shape[-1])
    arrived = lax.all_to_all(tiles, axis, split_axis=0, concat_axis=0, tiled=True)
    return jnp.sum(arrived.astype(jnp.float32), axis=0)


def per_device(queries, documents, candidates):
    local_docs, doc_len, width = documents.shape
    per_group, query_len, _ = queries.shape
    slots = candidates.shape[1]
    rows_of_y = lax.axis_size("y")
    groups = lax.axis_size(QG)
    total_queries = per_group * groups
    half_rows = total_queries * query_len // 2
    core = lax.axis_index("c")

    own = copy_for_each(queries, "y").reshape(half_rows, width)
    halves = [own, other_core(own)]

    def scored(rows):
        return sharpness_factor * lax.dot_general(
            rows, documents, (((1,), (2,)), ((), ())), preferred_element_type=jnp.float32
        )

    local_lse = []
    for rows in halves:
        part = scored(rows)
        peak = jnp.max(part, axis=2)
        mass = jnp.sum(jnp.exp(part - peak[:, :, None]), axis=2)
        local_lse.append(peak + jnp.log(mass))

    own_order = jnp.concatenate(local_lse).T.reshape(local_docs, 2, -1, 128)
    lse = jnp.where(core == 0, own_order, own_order[:, ::-1]).reshape(-1, 128)
    lse = log_of_sum(copy_for_each(lse, ("h", "l")))
    everyone = copy_for_each(lse, ("x", *QG))
    lse = log_of_sum(everyone.reshape(lax.axis_size("x"), -1, 128))
    lse, candidates, core, group = lax.optimization_barrier(
        (lse, candidates, core, lax.axis_index(QG))
    )

    all_docs = groups * local_docs
    scores = jnp.sum(lse.reshape(all_docs, total_queries, query_len), axis=2) / sharpness_factor
    by_core = candidates.reshape(rows_of_y, 2, per_group, slots).swapaxes(0, 1)
    by_core = by_core.reshape(total_queries, slots)
    picks = by_core[:, :, None] == jnp.arange(all_docs, dtype=jnp.int32)[None, None, :]
    pair = jnp.sum(jnp.where(picks, scores.T[:, None, :], 0.0), axis=2)
    highest = jnp.max(pair, axis=1, keepdims=True)
    total = highest + jnp.log(jnp.sum(jnp.exp(pair - highest), axis=1, keepdims=True))
    first = lax.broadcasted_iota(jnp.int32, pair.shape, 1) == 0
    dz = loss_scale / total_queries * (jnp.exp(pair - total) - jnp.where(first, 1.0, 0.0))
    owned = by_core[:, :, None] - group * local_docs == jnp.arange(local_docs, dtype=jnp.int32)
    weights = jnp.sum(jnp.where(owned, dz[:, :, None], 0.0), axis=1).reshape(2, -1, local_docs)
    weights = jnp.where(core == 0, weights, weights[::-1]).reshape(total_queries, local_docs)
    row_weight = jnp.repeat(weights, query_len, axis=0)
    mine = lax.dynamic_slice_in_dim(lse, group * len(own_order.reshape(-1, 128)), len(lse) // groups)
    mine = mine.reshape(own_order.shape)
    norm = jnp.where(core == 0, mine, mine[:, ::-1]).reshape(local_docs, -1).T

    def weighted_half(k):
        at = slice(k * half_rows, (k + 1) * half_rows)
        rows, this_norm, this_weight = lax.optimization_barrier(
            (halves[k], norm[at], row_weight[at])
        )
        prob = jnp.exp(scored(rows) - this_norm[:, :, None])
        return lax.optimization_barrier((this_weight[:, :, None] * prob).astype(jnp.bfloat16))

    def grad_of_rows(weighted):
        return lax.dot_general(
            weighted, documents, (((1, 2), (0, 1)), ((), ())), preferred_element_type=jnp.float32
        )

    theirs = weighted_half(1)
    received = other_core(grad_of_rows(theirs).astype(jnp.bfloat16))
    ours = weighted_half(0)
    chip = lax.optimization_barrier(grad_of_rows(ours)) + received.astype(jnp.float32)
    summed = sent_and_summed(chip, ("y", "x"))
    part = sent_and_summed(summed, ("h", "l")).astype(jnp.bfloat16)
    part, total, pair = lax.optimization_barrier((part, total, pair))
    loss = jnp.mean(total - pair[:, :1])
    grad_q = copy_for_each(part, CTX).reshape(queries.shape)
    grad_docs = sum(
        lax.dot_general(w, rows, (((0,), (0,)), ((), ())), preferred_element_type=jnp.float32)
        for w, rows in zip((ours, theirs), halves)
    ).astype(jnp.bfloat16)
    return loss, grad_q, grad_docs


def solution(mesh):
    finer = Mesh(mesh.devices.reshape(4, 4, 4, 4, 2), ("x", "h", "l", "y", "c"))
    in_specs = (P(QG, None, None), P(QG, CTX, None), P())
    out_specs = (P(), P(QG, None, None), P(QG, CTX, None))
    return jax.shard_map(
        per_device, mesh=finer, in_specs=in_specs, out_specs=out_specs, check_vma=False
    )
```

time: 146 us -> 137 us (0.938)
  blocking collectives: 41.6 us -> 80.3 us
  waiting for transfers between devices: 44.5 us -> 18.5 us
  starting transfers between devices: 33.2 us -> 16.7 us
  local copies, waits for them, and re-layouts: 7.78 us -> 4.23 us
  matrix products: 13.7 us -> 11.7 us
    all_to_all x2, blocking collectives: 24.5 us -> 46.3 us  [copy_for_each(): return lax.all_to_all(copies, axis, split_axis=0, concat_axis=0, tiled=True)]
    all_to_all x1 -> x2, blocking collectives: 17.1 us -> 34 us  [sent_and_summed(): lax.all_to_all(tiles, axis, split_axis=0, concat_axis=0, tiled=True)]
    all_to_all x3 -> x2, starting transfers between devices: 25.6 us -> 12.7 us  [copy_for_each(): return lax.all_to_all(copies, axis, split_axis=0, concat_axis=0, tiled=True)]
    all_to_all x3 -> x2, waiting for transfers between devices: 30.1 us -> 17.6 us  [copy_for_each(): return lax.all_to_all(copies, axis, split_axis=0, concat_axis=0, tiled=True)]
    all_to_all x1 -> x0, waiting for transfers between devices: 12.1 us -> none  [sent_and_summed(): lax.all_to_all(tiles, axis, split_axis=0, concat_axis=0, tiled=True)]
    all_to_all x1 -> x0, starting transfers between devices: 3.79 us -> none  [sent_and_summed(): lax.all_to_all(tiles, axis, split_axis=0, concat_axis=0, tiled=True)]
    dot_general x2, matrix products: 6.5 us -> 2.95 us  [grad_of_rows(): lax.dot_general(weighted, documents, (((1, 2), (0, 1)), ((), ())), prefer...]
    unnamed x14, local copies, waits for them, and re-layouts: 2.28 us -> 0.04 us
  transfers between devices with their start and end apart: 6 -> 4, of which waited for: 5 -> 3; matrix products, arithmetic and copies ran while one was open for 5% -> 6% of each run, Pallas kernels for 0% -> 0%
where the time goes in v3:
time: 137 us; the launch traced here: 136 us
  blocking collectives  80.3 us (59%)
  waiting for transfers between devices  18.5 us (14%)
  starting transfers between devices  16.7 us (12%)
  matrix products  11.7 us (9%)
  local copies, waits for them, and re-layouts  4.23 us (3%)
  between operations  2.76 us (2%)
  other arithmetic  2.22 us (2%)
    all_to_all x2, blocking collectives, copy_for_each(): return lax.all_to_all(copies, axis, split_axis=0, concat_axis=0, tiled=True)  46.3 us
    all_to_all x2, blocking collectives, sent_and_summed(): lax.all_to_all(tiles, axis, split_axis=0, concat_axis=0, tiled=True)  34 us
    all_to_all x2, waiting for transfers between devices, copy_for_each(): return lax.all_to_all(copies, axis, split_axis=0, concat_axis=0, tiled=True)  17.6 us
    all_to_all x2, starting transfers between devices, copy_for_each(): return lax.all_to_all(copies, axis, split_axis=0, concat_axis=0, tiled=True)  12.7 us
    dot_general x2, matrix products, per_device(): lax.dot_general(w, rows, (((0,), (0,)), ((), ())), preferred_element_type...  4.46 us
    dot_general x4, matrix products, scored(): lax.dot_general(rows, documents, (((1,), (2,)), ((), ())), preferred_elem...  4.29 us
    ppermute x2, starting transfers between devices, other_core(): return lax.ppermute(x, 'c', [(0, 1), (1, 0)])  4.09 us
    dot_general x2, matrix products, grad_of_rows(): lax.dot_general(weighted, documents, (((1, 2), (0, 1)), ((), ())), prefer...  2.95 us
  transfers between devices with their start and end apart: 4, of which 3 were waited for; matrix products, arithmetic and copies ran while one was open for 6% of the time, Pallas kernels for 0%

profile of v3, /device:TPU:6, one launch (start us, length us, event | category | flops | bytes accessed | tf_op | source)
XLA Modules:
  0.0 136.4 jit_solution(10730015814870317912)
XLA Ops:
  0.6 1.1 broadcast_in_dim.63
  1.8 16.6 %all_to_all.30 = bf16[4,4,32,768]{3,2,1,0:T(8,128)(2,1)S(1)} all-to-all(bf16[4,4,32,768]{3,2,1,0:T(8,128)(2,1)S(1)} %broadcast_in_dim.63), channel_id=1, replica_groups=mesh['x'=4,'h'=4,'l'=4,'y'=4,'c'=2] {'y'}, dimensions={0} | all-to-all | bytes 1572864 | tf_op jit(solution)/shard_map/all_to_all | solution.py:16
  18.3 1.9 %collective-permute-start = (bf16[512,768]{1,0:T(8,128)(2,1)S(1)}, bf16[512,768]{1,0:T(8,128)(2,1)S(1)}, u32[]{:S(2)}, u32[]{:S(2)}) collective-permute-start(bf16[512,768]{1,0:T(8,128)(2,1)S(1)} %bitcast.65), channel_id=1, source_target_pairs={{0,1},{1,0},{2,3},{3,2},{4,5},{5,4},{6,7},{7,6},{8,9},{9,8},{10,11... | collective-permute-start | bytes 2359304 | tf_op jit(solution)/shard_map/ppermute | solution.py:20
  20.3 1.0 multiply_reduce_fusion.1
  21.3 0.4 exponential_reduce_fusion.1
  21.6 0.8 collective-permute-done
  22.5 1.0 multiply_reduce_fusion
  23.5 0.4 exponential_reduce_fusion
  24.0 29.7 %all_to_all.31 = f32[16,16,128]{2,1,0:T(8,128)S(1)} all-to-all(f32[16,16,128]{2,1,0:T(8,128)S(1)} %broadcast_in_dim.64), channel_id=1, replica_groups=mesh['x'=4,'h'=4,'l'=4,'y'=4,'c'=2] {'h','l'}, dimensions={0} | all-to-all | bytes 262144 | tf_op jit(solution)/shard_map/all_to_all | solution.py:16
  53.8 0.7 broadcast_in_dim.65
  54.5 5.6 %all-to-all-start.2 = ((f32[32,16,128]{2,1,0:T(8,128)}), f32[32,16,128]{2,1,0:T(8,128)S(1)}, u32[]{:S(2)}, u32[]{:S(2)}) async-start(f32[32,16,128]{2,1,0:T(8,128)} %broadcast_in_dim.65), calls=%async_computation.2 | async-start | bytes 524288 | tf_op jit(solution)/shard_map/all_to_all | solution.py:16
  60.1 6.9 %all-to-all-done.2 = f32[32,16,128]{2,1,0:T(8,128)S(1)} async-done(((f32[32,16,128]{2,1,0:T(8,128)}), f32[32,16,128]{2,1,0:T(8,128)S(1)}, u32[]{:S(2)}, u32[]{:S(2)}) %all-to-all-start.2) | async-done | bytes 262176 | tf_op jit(solution)/shard_map/all_to_all | solution.py:16
  67.2 0.1 reshape.120
  67.3 0.1 reshape.119
  67.5 0.1 broadcast_in_dim_reshape.4
  67.5 0.1 reduce_sum.109
  68.2 1.1 multiply_convert_fusion
  69.3 1.9 %bitcast_convert_fusion = bf16[512,768]{1,0:T(8,128)(2,1)} fusion(bf16[512,2,512]{0,2,1:T(8,128)(2,1)S(1)} %multiply_convert_fusion, bf16[2,512,768]{2,1,0:T(8,128)(2,1)S(1)} %copy-done), kind=kOutput, calls=%fused_computation.7 | convolution fusion | flops 805699584 | bytes 3407872 | tf_op jit(solution)/shard_map/dot_general | solution.py:95
  71.3 2.2 %collective-permute-start.1 = (bf16[512,768]{1,0:T(8,128)(2,1)}, bf16[512,768]{1,0:T(8,128)(2,1)S(1)}, u32[]{:S(2)}, u32[]{:S(2)}) collective-permute-start(bf16[512,768]{1,0:T(8,128)(2,1)} %bitcast_convert_fusion), channel_id=1, source_target_pairs={{0,1},{1,0},{2,3},{3,2},{4,5},{5,4},{6,7},{7,6},{8,9},{9,8},{10,11... | collective-permute-start | bytes 2359304 | tf_op jit(solution)/shard_map/ppermute | solution.py:20
  73.6 1.1 multiply_convert_fusion.1
  74.7 1.0 convolution_bitcast_fusion
  75.8 0.2 add_convert_fusion.1
  76.0 17.4 %all_to_all.32 = bf16[16,32,768]{2,1,0:T(8,128)(2,1)S(1)} all-to-all(bf16[16,32,768]{2,1,0:T(8,128)(2,1)S(1)} %bitcast.69), channel_id=1, replica_groups=mesh['x'=4,'h'=4,'l'=4,'y'=4,'c'=2] {'y','x'}, dimensions={0} | all-to-all | bytes 1572864 | tf_op jit(solution)/shard_map/all_to_all | solution.py:30
  93.4 0.1 reduce_sum.113
  93.6 16.6 %all_to_all.33 = bf16[16,2,768]{2,1,0:T(2,128)(2,1)S(1)} all-to-all(bf16[16,2,768]{2,1,0:T(2,128)(2,1)S(1)} %reshape.123), channel_id=1, replica_groups=mesh['x'=4,'h'=4,'l'=4,'y'=4,'c'=2] {'h','l'}, dimensions={0} | all-to-all | bytes 98304 | tf_op jit(solution)/shard_map/all_to_all | solution.py:30
  110.2 0.8 broadcast_in_dim.74
  111.0 7.1 %all-to-all-start.5 = ((bf16[64,2,768]{2,1,0:T(2,128)(2,1)}), bf16[64,2,768]{2,1,0:T(2,128)(2,1)S(1)}, u32[]{:S(2)}, u32[]{:S(2)}) async-start(bf16[64,2,768]{2,1,0:T(2,128)(2,1)} %broadcast_in_dim.74), calls=%async_computation.5 | async-start | bytes 393216 | tf_op jit(solution)/shard_map/all_to_all | solution.py:16
  118.1 2.3 %fusion.12 = f32[2,512,768]{2,1,0:T(8,128)S(1)} fusion(bf16[512,2,512]{0,2,1:T(8,128)(2,1)} %copy-done.3, bf16[512,768,1]{1,0,2:T(8,128)(2,1)S(1)} %bitcast.68), kind=kOutput, calls=%fused_computation.43 | convolution fusion | flops 805306368 | bytes 4980736 | tf_op jit(solution)/shard_map/dot_general | solution.py:109
  120.5 2.1 %add_convert_fusion = bf16[2,512,768]{2,1,0:T(8,128)(2,1)} fusion(f32[2,512,768]{2,1,0:T(8,128)S(1)} %fusion.12, bf16[512,2,512]{0,2,1:T(8,128)(2,1)S(1)} %copy-done.2, bf16[512,768]{1,0:T(8,128)(2,1)S(1)} %copy-done.5), kind=kOutput, calls=%fused_computation | convolution fusion | flops 806879232 | bytes 6553600 | tf_op jit(solution)/shard_map/dot_general | solution.py:109
  122.6 0.6 subtract_reduce_fusion
  123.9 10.7 %all-to-all-done.5 = bf16[64,2,768]{2,1,0:T(2,128)(2,1)S(1)} async-done(((bf16[64,2,768]{2,1,0:T(2,128)(2,1)}), bf16[64,2,768]{2,1,0:T(2,128)(2,1)S(1)}, u32[]{:S(2)}, u32[]{:S(2)}) %all-to-all-start.5) | async-done | bytes 196640 | tf_op jit(solution)/shard_map/all_to_all | solution.py:16
  134.6 0.8 reshape.124
  (50 shorter events, 1.0 us)
Async XLA Ops:
  0.6 19.6 %copy-start = (bf16[2,512,768]{2,1,0:T(8,128)(2,1)S(1)}, bf16[2,512,768]{2,1,0:T(8,128)(2,1)}, u32[]{:S(2)}) copy-start(bf16[2,512,768]{2,1,0:T(8,128)(2,1)} %param.4) | copy-start | bytes 4718596
  18.3 4.2 %collective-permute-start = (bf16[512,768]{1,0:T(8,128)(2,1)S(1)}, bf16[512,768]{1,0:T(8,128)(2,1)S(1)}, u32[]{:S(2)}, u32[]{:S(2)}) collective-permute-start(bf16[512,768]{1,0:T(8,128)(2,1)S(1)} %bitcast.65), channel_id=1, source_target_pairs={{0,1},{1,0},{2,3},{3,2},{4,5},{5,4},{6,7},{7,6},{8,9},{9,8},{10,11... | collective-permute-start | bytes 2359304 | tf_op jit(solution)/shard_map/ppermute | solution.py:20
  22.5 45.7 %copy-start.4 = (bf16[512,768]{1,0:T(8,128)(2,1)}, bf16[512,768]{1,0:T(8,128)(2,1)S(1)}, u32[]{:S(2)}) copy-start(bf16[512,768]{1,0:T(8,128)(2,1)S(1)} %collective-permute-done) | copy-start | bytes 2359300
  23.5 43.8 %copy-start.6 = (s32[32,4]{0,1:T(4,128)S(1)}, s32[32,4]{0,1:T(4,128)}, u32[]{:S(2)}) copy-start(s32[32,4]{0,1:T(4,128)} %param.5) | copy-start | bytes 1540
  54.5 12.6 %all-to-all-start.2 = ((f32[32,16,128]{2,1,0:T(8,128)}), f32[32,16,128]{2,1,0:T(8,128)S(1)}, u32[]{:S(2)}, u32[]{:S(2)}) async-start(f32[32,16,128]{2,1,0:T(8,128)} %broadcast_in_dim.65), calls=%async_computation.2 | async-start | bytes 524288 | tf_op jit(solution)/shard_map/all_to_all | solution.py:16
  69.3 1.9 %copy-start.1 = (bf16[512,2,512]{0,2,1:T(8,128)(2,1)}, bf16[512,2,512]{0,2,1:T(8,128)(2,1)S(1)}, u32[]{:S(2)}) copy-start(bf16[512,2,512]{0,2,1:T(8,128)(2,1)S(1)} %multiply_convert_fusion) | copy-start | bytes 3145732
  71.3 4.5 %collective-permute-start.1 = (bf16[512,768]{1,0:T(8,128)(2,1)}, bf16[512,768]{1,0:T(8,128)(2,1)S(1)}, u32[]{:S(2)}, u32[]{:S(2)}) collective-permute-start(bf16[512,768]{1,0:T(8,128)(2,1)} %bitcast_convert_fusion), channel_id=1, source_target_pairs={{0,1},{1,0},{2,3},{3,2},{4,5},{5,4},{6,7},{7,6},{8,9},{9,8},{10,11... | collective-permute-start | bytes 2359304 | tf_op jit(solution)/shard_map/ppermute | solution.py:20
  74.7 1.1 copy-start.3
  111.0 23.5 %all-to-all-start.5 = ((bf16[64,2,768]{2,1,0:T(2,128)(2,1)}), bf16[64,2,768]{2,1,0:T(2,128)(2,1)S(1)}, u32[]{:S(2)}, u32[]{:S(2)}) async-start(bf16[64,2,768]{2,1,0:T(2,128)(2,1)} %broadcast_in_dim.74), calls=%async_computation.5 | async-start | bytes 393216 | tf_op jit(solution)/shard_map/all_to_all | solution.py:16
  118.1 2.4 %copy-start.2 = (bf16[512,2,512]{0,2,1:T(8,128)(2,1)S(1)}, bf16[512,2,512]{0,2,1:T(8,128)(2,1)}, u32[]{:S(2)}) copy-start(bf16[512,2,512]{0,2,1:T(8,128)(2,1)} %copy-done.1) | copy-start | bytes 3145732
  118.1 2.4 %copy-start.5 = (bf16[512,768]{1,0:T(8,128)(2,1)S(1)}, bf16[512,768]{1,0:T(8,128)(2,1)}, u32[]{:S(2)}) copy-start(bf16[512,768]{1,0:T(8,128)(2,1)} %copy-done.4) | copy-start | bytes 2359300

commit v4 on v3

--- a/solution.py
+++ b/solution.py
@@ -101,10 +101,13 @@
     ours = weighted_half(0)
     chip = lax.optimization_barrier(grad_of_rows(ours)) + received.astype(jnp.float32)
     summed = sent_and_summed(chip, ("y", "x"))
-    part = sent_and_summed(summed, ("h", "l")).astype(jnp.bfloat16)
+    near = summed.astype(jnp.bfloat16).reshape(lax.axis_size("l"), -1, width)
+    tiles = jnp.broadcast_to(near, (lax.axis_size("h"), *near.shape)).reshape(-1, *near.shape[1:])
+    arrived = lax.all_to_all(tiles, ("h", "l"), split_axis=0, concat_axis=0, tiled=True)
+    part = jnp.sum(arrived.astype(jnp.float32), axis=0).astype(jnp.bfloat16)
     part, total, pair = lax.optimization_barrier((part, total, pair))
     loss = jnp.mean(total - pair[:, :1])
-    grad_q = copy_for_each(part, CTX).reshape(queries.shape)
+    grad_q = copy_for_each(part, ("x", "l")).reshape(queries.shape)
     grad_docs = sum(
         lax.dot_general(w, rows, (((0,), (0,)), ((), ())), preferred_element_type=jnp.float32)
         for w, rows in zip((ours, theirs), halves)

time: 137 us -> 131 us (0.956)
  waiting for transfers between devices: 18.5 us -> 8.72 us
  blocking collectives: 80.3 us -> 83.4 us
    all_to_all x0 -> x1, blocking collectives: none -> 19.7 us  [per_device(): lax.all_to_all(tiles, ('h', 'l'), split_axis=0, concat_axis=0, tiled=True)]
    all_to_all x2 -> x1, blocking collectives: 34 us -> 17.4 us  [sent_and_summed(): lax.all_to_all(tiles, axis, split_axis=0, concat_axis=0, tiled=True)]
    all_to_all x2, waiting for transfers between devices: 17.6 us -> 7.88 us  [copy_for_each(): return lax.all_to_all(copies, axis, split_axis=0, concat_axis=0, tiled=True)]
  transfers between devices with their start and end apart: 4 -> 4, of which waited for: 3 -> 3; matrix products, arithmetic and copies ran while one was open for 6% -> 7% of each run, Pallas kernels for 0% -> 0%
where the time goes in v4:
time: 131 us; the launch traced here: 130 us
  blocking collectives  83.4 us (64%)
  starting transfers between devices  17.1 us (13%)
  matrix products  11.7 us (9%)
  waiting for transfers between devices  8.72 us (7%)
  local copies, waits for them, and re-layouts  4.05 us (3%)
  between operations  2.76 us (2%)
  other arithmetic  2.2 us (2%)
    all_to_all x2, blocking collectives, copy_for_each(): return lax.all_to_all(copies, axis, split_axis=0, concat_axis=0, tiled=True)  46.3 us
    all_to_all x1, blocking collectives, per_device(): lax.all_to_all(tiles, ('h', 'l'), split_axis=0, concat_axis=0, tiled=True)  19.7 us
    all_to_all x1, blocking collectives, sent_and_summed(): lax.all_to_all(tiles, axis, split_axis=0, concat_axis=0, tiled=True)  17.4 us
    all_to_all x2, starting transfers between devices, copy_for_each(): return lax.all_to_all(copies, axis, split_axis=0, concat_axis=0, tiled=True)  13 us
    all_to_all x2, waiting for transfers between devices, copy_for_each(): return lax.all_to_all(copies, axis, split_axis=0, concat_axis=0, tiled=True)  7.88 us
    dot_general x2, matrix products, per_device(): lax.dot_general(w, rows, (((0,), (0,)), ((), ())), preferred_element_type...  4.46 us
    dot_general x4, matrix products, scored(): lax.dot_general(rows, documents, (((1,), (2,)), ((), ())), preferred_elem...  4.29 us
    ppermute x2, starting transfers between devices, other_core(): return lax.ppermute(x, 'c', [(0, 1), (1, 0)])  4.09 us
  transfers between devices with their start and end apart: 4, of which 3 were waited for; matrix products, arithmetic and copies ran while one was open for 7% of the time, Pallas kernels for 0%

profile of v4, /device:TPU:6, one launch (start us, length us, event | category | flops | bytes accessed | tf_op | source)
XLA Modules:
  0.0 129.9 jit_solution(12891240503918044715)
XLA Ops:
  0.6 1.1 broadcast_in_dim.66
  1.8 16.6 %all_to_all.30 = bf16[4,4,32,768]{3,2,1,0:T(8,128)(2,1)S(1)} all-to-all(bf16[4,4,32,768]{3,2,1,0:T(8,128)(2,1)S(1)} %broadcast_in_dim.66), channel_id=1, replica_groups=mesh['x'=4,'h'=4,'l'=4,'y'=4,'c'=2] {'y'}, dimensions={0} | all-to-all | bytes 1572864 | tf_op jit(solution)/shard_map/all_to_all | solution.py:16
  18.3 1.9 %collective-permute-start = (bf16[512,768]{1,0:T(8,128)(2,1)S(1)}, bf16[512,768]{1,0:T(8,128)(2,1)S(1)}, u32[]{:S(2)}, u32[]{:S(2)}) collective-permute-start(bf16[512,768]{1,0:T(8,128)(2,1)S(1)} %bitcast.68), channel_id=1, source_target_pairs={{0,1},{1,0},{2,3},{3,2},{4,5},{5,4},{6,7},{7,6},{8,9},{9,8},{10,11... | collective-permute-start | bytes 2359304 | tf_op jit(solution)/shard_map/ppermute | solution.py:20
  20.3 1.0 multiply_reduce_fusion.1
  21.3 0.4 exponential_reduce_fusion.1
  21.6 0.8 collective-permute-done
  22.5 1.0 multiply_reduce_fusion
  23.5 0.4 exponential_reduce_fusion
  24.0 29.7 %all_to_all.31 = f32[16,16,128]{2,1,0:T(8,128)S(1)} all-to-all(f32[16,16,128]{2,1,0:T(8,128)S(1)} %broadcast_in_dim.67), channel_id=1, replica_groups=mesh['x'=4,'h'=4,'l'=4,'y'=4,'c'=2] {'h','l'}, dimensions={0} | all-to-all | bytes 262144 | tf_op jit(solution)/shard_map/all_to_all | solution.py:16
  53.8 0.7 broadcast_in_dim.68
  54.5 5.6 %all-to-all-start.2 = ((f32[32,16,128]{2,1,0:T(8,128)}), f32[32,16,128]{2,1,0:T(8,128)S(1)}, u32[]{:S(2)}, u32[]{:S(2)}) async-start(f32[32,16,128]{2,1,0:T(8,128)} %broadcast_in_dim.68), calls=%async_computation.2 | async-start | bytes 524288 | tf_op jit(solution)/shard_map/all_to_all | solution.py:16
  60.1 6.9 %all-to-all-done.2 = f32[32,16,128]{2,1,0:T(8,128)S(1)} async-done(((f32[32,16,128]{2,1,0:T(8,128)}), f32[32,16,128]{2,1,0:T(8,128)S(1)}, u32[]{:S(2)}, u32[]{:S(2)}) %all-to-all-start.2) | async-done | bytes 262176 | tf_op jit(solution)/shard_map/all_to_all | solution.py:16
  67.2 0.1 reshape.123
  67.3 0.1 reshape.122
  67.5 0.1 broadcast_in_dim_reshape.4
  67.5 0.1 reduce_sum.109
  68.2 1.1 multiply_convert_fusion
  69.3 1.9 %bitcast_convert_fusion = bf16[512,768]{1,0:T(8,128)(2,1)} fusion(bf16[512,2,512]{0,2,1:T(8,128)(2,1)S(1)} %multiply_convert_fusion, bf16[2,512,768]{2,1,0:T(8,128)(2,1)S(1)} %copy-done), kind=kOutput, calls=%fused_computation.7 | convolution fusion | flops 805699584 | bytes 3407872 | tf_op jit(solution)/shard_map/dot_general | solution.py:95
  71.3 2.2 %collective-permute-start.1 = (bf16[512,768]{1,0:T(8,128)(2,1)}, bf16[512,768]{1,0:T(8,128)(2,1)S(1)}, u32[]{:S(2)}, u32[]{:S(2)}) collective-permute-start(bf16[512,768]{1,0:T(8,128)(2,1)} %bitcast_convert_fusion), channel_id=1, source_target_pairs={{0,1},{1,0},{2,3},{3,2},{4,5},{5,4},{6,7},{7,6},{8,9},{9,8},{10,11... | collective-permute-start | bytes 2359304 | tf_op jit(solution)/shard_map/ppermute | solution.py:20
  73.6 1.1 multiply_convert_fusion.1
  74.7 1.0 convolution_bitcast_fusion
  75.8 0.2 add_convert_fusion.1
  76.0 17.4 %all_to_all.32 = bf16[16,32,768]{2,1,0:T(8,128)(2,1)S(1)} all-to-all(bf16[16,32,768]{2,1,0:T(8,128)(2,1)S(1)} %bitcast.72), channel_id=1, replica_groups=mesh['x'=4,'h'=4,'l'=4,'y'=4,'c'=2] {'y','x'}, dimensions={0} | all-to-all | bytes 1572864 | tf_op jit(solution)/shard_map/all_to_all | solution.py:30
  93.4 0.1 reduce_sum.113
  93.6 19.7 %all_to_all.33 = bf16[16,8,768]{2,1,0:T(8,128)(2,1)S(1)} all-to-all(bf16[16,8,768]{2,1,0:T(8,128)(2,1)S(1)} %bitcast.76), channel_id=1, replica_groups=mesh['x'=4,'h'=4,'l'=4,'y'=4,'c'=2] {'h','l'}, dimensions={0} | all-to-all | bytes 393216 | tf_op jit(solution)/shard_map/all_to_all | solution.py:106
  113.3 0.7 broadcast_in_dim.78
  114.0 7.4 %all-to-all-start.5 = ((bf16[16,8,768]{2,1,0:T(8,128)(2,1)}), bf16[16,8,768]{2,1,0:T(8,128)(2,1)S(1)}, u32[]{:S(2)}, u32[]{:S(2)}) async-start(bf16[16,8,768]{2,1,0:T(8,128)(2,1)} %broadcast_in_dim.78), calls=%async_computation.5 | async-start | bytes 393216 | tf_op jit(solution)/shard_map/all_to_all | solution.py:16
  121.4 2.3 %fusion.12 = f32[2,512,768]{2,1,0:T(8,128)S(1)} fusion(bf16[512,2,512]{0,2,1:T(8,128)(2,1)} %copy-done.3, bf16[512,768,1]{1,0,2:T(8,128)(2,1)S(1)} %bitcast.71), kind=kOutput, calls=%fused_computation.43 | convolution fusion | flops 805306368 | bytes 4980736 | tf_op jit(solution)/shard_map/dot_general | solution.py:112
  123.8 2.1 %add_convert_fusion = bf16[2,512,768]{2,1,0:T(8,128)(2,1)} fusion(f32[2,512,768]{2,1,0:T(8,128)S(1)} %fusion.12, bf16[512,2,512]{0,2,1:T(8,128)(2,1)S(1)} %copy-done.2, bf16[512,768]{1,0:T(8,128)(2,1)S(1)} %copy-done.5), kind=kOutput, calls=%fused_computation | convolution fusion | flops 806879232 | bytes 6553600 | tf_op jit(solution)/shard_map/dot_general | solution.py:112
  125.9 0.6 subtract_reduce_fusion
  127.2 0.9 all-to-all-done.5
  128.1 0.7 copy.33
  (50 shorter events, 1.0 us)
Async XLA Ops:
  0.6 19.6 %copy-start = (bf16[2,512,768]{2,1,0:T(8,128)(2,1)S(1)}, bf16[2,512,768]{2,1,0:T(8,128)(2,1)}, u32[]{:S(2)}) copy-start(bf16[2,512,768]{2,1,0:T(8,128)(2,1)} %param.4) | copy-start | bytes 4718596
  18.3 4.2 %collective-permute-start = (bf16[512,768]{1,0:T(8,128)(2,1)S(1)}, bf16[512,768]{1,0:T(8,128)(2,1)S(1)}, u32[]{:S(2)}, u32[]{:S(2)}) collective-permute-start(bf16[512,768]{1,0:T(8,128)(2,1)S(1)} %bitcast.68), channel_id=1, source_target_pairs={{0,1},{1,0},{2,3},{3,2},{4,5},{5,4},{6,7},{7,6},{8,9},{9,8},{10,11... | collective-permute-start | bytes 2359304 | tf_op jit(solution)/shard_map/ppermute | solution.py:20
  22.5 45.7 %copy-start.4 = (bf16[512,768]{1,0:T(8,128)(2,1)}, bf16[512,768]{1,0:T(8,128)(2,1)S(1)}, u32[]{:S(2)}) copy-start(bf16[512,768]{1,0:T(8,128)(2,1)S(1)} %collective-permute-done) | copy-start | bytes 2359300
  23.5 43.8 %copy-start.6 = (s32[32,4]{0,1:T(4,128)S(1)}, s32[32,4]{0,1:T(4,128)}, u32[]{:S(2)}) copy-start(s32[32,4]{0,1:T(4,128)} %param.5) | copy-start | bytes 1540
  54.5 12.6 %all-to-all-start.2 = ((f32[32,16,128]{2,1,0:T(8,128)}), f32[32,16,128]{2,1,0:T(8,128)S(1)}, u32[]{:S(2)}, u32[]{:S(2)}) async-start(f32[32,16,128]{2,1,0:T(8,128)} %broadcast_in_dim.68), calls=%async_computation.2 | async-start | bytes 524288 | tf_op jit(solution)/shard_map/all_to_all | solution.py:16
  69.3 1.9 %copy-start.1 = (bf16[512,2,512]{0,2,1:T(8,128)(2,1)}, bf16[512,2,512]{0,2,1:T(8,128)(2,1)S(1)}, u32[]{:S(2)}) copy-start(bf16[512,2,512]{0,2,1:T(8,128)(2,1)S(1)} %multiply_convert_fusion) | copy-start | bytes 3145732
  71.3 4.5 %collective-permute-start.1 = (bf16[512,768]{1,0:T(8,128)(2,1)}, bf16[512,768]{1,0:T(8,128)(2,1)S(1)}, u32[]{:S(2)}, u32[]{:S(2)}) collective-permute-start(bf16[512,768]{1,0:T(8,128)(2,1)} %bitcast_convert_fusion), channel_id=1, source_target_pairs={{0,1},{1,0},{2,3},{3,2},{4,5},{5,4},{6,7},{7,6},{8,9},{9,8},{10,11... | collective-permute-start | bytes 2359304 | tf_op jit(solution)/shard_map/ppermute | solution.py:20
  74.7 1.1 copy-start.3
  114.0 14.1 %all-to-all-start.5 = ((bf16[16,8,768]{2,1,0:T(8,128)(2,1)}), bf16[16,8,768]{2,1,0:T(8,128)(2,1)S(1)}, u32[]{:S(2)}, u32[]{:S(2)}) async-start(bf16[16,8,768]{2,1,0:T(8,128)(2,1)} %broadcast_in_dim.78), calls=%async_computation.5 | async-start | bytes 393216 | tf_op jit(solution)/shard_map/all_to_all | solution.py:16
  121.4 2.4 %copy-start.2 = (bf16[512,2,512]{0,2,1:T(8,128)(2,1)S(1)}, bf16[512,2,512]{0,2,1:T(8,128)(2,1)}, u32[]{:S(2)}) copy-start(bf16[512,2,512]{0,2,1:T(8,128)(2,1)} %copy-done.1) | copy-start | bytes 3145732
  121.4 2.4 %copy-start.5 = (bf16[512,768]{1,0:T(8,128)(2,1)S(1)}, bf16[512,768]{1,0:T(8,128)(2,1)}, u32[]{:S(2)}) copy-start(bf16[512,768]{1,0:T(8,128)(2,1)} %copy-done.4) | copy-start | bytes 2359300

commit v5 on v3

--- a/solution.py
+++ b/solution.py
@@ -5,7 +5,7 @@
 from jax.sharding import PartitionSpec as P
 
 QG = ("y", "c")
-CTX = ("x", "h", "l")
+CTX = ("x", "h", "m", "p")
 
 sharpness_factor = 2.0
 loss_scale = 1024.0
@@ -14,6 +14,13 @@
 def copy_for_each(x, axis):
     copies = jnp.broadcast_to(x, (lax.axis_size(axis), *x.shape))
     return lax.all_to_all(copies, axis, split_axis=0, concat_axis=0, tiled=True)
+
+
+def shared_and_scattered(x, far, near):
+    tiles = x.reshape(lax.axis_size(near), -1, x.shape[-1])
+    copies = jnp.broadcast_to(tiles, (lax.axis_size(far), *tiles.shape))
+    copies = copies.reshape(-1, *tiles.shape[1:])
+    return lax.all_to_all(copies, (*far, near), split_axis=0, concat_axis=0, tiled=True)
 
 
 def other_core(x):
@@ -58,8 +65,8 @@
 
     own_order = jnp.concatenate(local_lse).T.reshape(local_docs, 2, -1, 128)
     lse = jnp.where(core == 0, own_order, own_order[:, ::-1]).reshape(-1, 128)
-    lse = log_of_sum(copy_for_each(lse, ("h", "l")))
-    everyone = copy_for_each(lse, ("x", *QG))
+    lse = log_of_sum(shared_and_scattered(lse, ("h", "m"), "p"))
+    everyone = copy_for_each(lse, ("x", *QG, "p"))
     lse = log_of_sum(everyone.reshape(lax.axis_size("x"), -1, 128))
     lse, candidates, core, group = lax.optimization_barrier(
         (lse, candidates, core, lax.axis_index(QG))
@@ -100,11 +107,12 @@
     received = other_core(grad_of_rows(theirs).astype(jnp.bfloat16))
     ours = weighted_half(0)
     chip = lax.optimization_barrier(grad_of_rows(ours)) + received.astype(jnp.float32)
-    summed = sent_and_summed(chip, ("y", "x"))
-    part = sent_and_summed(summed, ("h", "l")).astype(jnp.bfloat16)
+    summed = sent_and_summed(chip, ("y", "x", "p"))
+    arrived = shared_and_scattered(summed.astype(jnp.bfloat16), ("h",), "m")
+    part = jnp.sum(arrived.astype(jnp.float32), axis=0).astype(jnp.bfloat16)
     part, total, pair = lax.optimization_barrier((part, total, pair))
     loss = jnp.mean(total - pair[:, :1])
-    grad_q = copy_for_each(part, CTX).reshape(queries.shape)
+    grad_q = copy_for_each(part, ("x", "p", "m")).reshape(queries.shape)
     grad_docs = sum(
         lax.dot_general(w, rows, (((0,), (0,)), ((), ())), preferred_element_type=jnp.float32)
         for w, rows in zip((ours, theirs), halves)
@@ -113,7 +121,7 @@
 
 
 def solution(mesh):
-    finer = Mesh(mesh.devices.reshape(4, 4, 4, 4, 2), ("x", "h", "l", "y", "c"))
+    finer = Mesh(mesh.devices.reshape(4, 4, 2, 2, 4, 2), ("x", "h", "m", "p", "y", "c"))
     in_specs = (P(QG, None, None), P(QG, CTX, None), P())
     out_specs = (P(), P(QG, None, None), P(QG, CTX, None))
     return jax.shard_map(

time: 137 us -> 128 us (0.934)
  waiting for transfers between devices: 18.5 us -> 9.76 us
    all_to_all x0 -> x2, blocking collectives: none -> 45.8 us  [shared_and_scattered(): lax.all_to_all(copies, (*far, near), split_axis=0, concat_axis=0, tiled=T...]
    all_to_all x2 -> x1, blocking collectives: 46.3 us -> 16.6 us  [copy_for_each(): return lax.all_to_all(copies, axis, split_axis=0, concat_axis=0, tiled=True)]
    all_to_all x2 -> x1, blocking collectives: 34 us -> 18.5 us  [sent_and_summed(): lax.all_to_all(tiles, axis, split_axis=0, concat_axis=0, tiled=True)]
    all_to_all x2, waiting for transfers between devices: 17.6 us -> 8.81 us  [copy_for_each(): return lax.all_to_all(copies, axis, split_axis=0, concat_axis=0, tiled=True)]
  transfers between devices with their start and end apart: 4 -> 4, of which waited for: 3 -> 4; matrix products, arithmetic and copies ran while one was open for 6% -> 7% of each run, Pallas kernels for 0% -> 0%
where the time goes in v5:
time: 128 us; the launch traced here: 127 us
  blocking collectives  80.8 us (63%)
  starting transfers between devices  15.9 us (12%)
  matrix products  11.7 us (9%)
  waiting for transfers between devices  9.76 us (8%)
  local copies, waits for them, and re-layouts  4.04 us (3%)
  between operations  2.74 us (2%)
  other arithmetic  2.18 us (2%)
    all_to_all x2, blocking collectives, shared_and_scattered(): lax.all_to_all(copies, (*far, near), split_axis=0, concat_axis=0, tiled=T...  45.8 us
    all_to_all x1, blocking collectives, sent_and_summed(): lax.all_to_all(tiles, axis, split_axis=0, concat_axis=0, tiled=True)  18.5 us
    all_to_all x1, blocking collectives, copy_for_each(): return lax.all_to_all(copies, axis, split_axis=0, concat_axis=0, tiled=True)  16.6 us
    all_to_all x2, starting transfers between devices, copy_for_each(): return lax.all_to_all(copies, axis, split_axis=0, concat_axis=0, tiled=True)  12.1 us
    all_to_all x2, waiting for transfers between devices, copy_for_each(): return lax.all_to_all(copies, axis, split_axis=0, concat_axis=0, tiled=True)  8.81 us
    dot_general x2, matrix products, per_device(): lax.dot_general(w, rows, (((0,), (0,)), ((), ())), preferred_element_type...  4.46 us
    dot_general x4, matrix products, scored(): lax.dot_general(rows, documents, (((1,), (2,)), ((), ())), preferred_elem...  4.3 us
    ppermute x2, starting transfers between devices, other_core(): return lax.ppermute(x, 'c', [(0, 1), (1, 0)])  3.82 us
  transfers between devices with their start and end apart: 4, of which 4 were waited for; matrix products, arithmetic and copies ran while one was open for 7% of the time, Pallas kernels for 0%

profile of v5, /device:TPU:6, one launch (start us, length us, event | category | flops | bytes accessed | tf_op | source)
XLA Modules:
  0.0 127.2 jit_solution(5508260856780280801)
XLA Ops:
  0.6 1.1 broadcast_in_dim.66
  1.8 16.6 %all_to_all.30 = bf16[4,4,32,768]{3,2,1,0:T(8,128)(2,1)S(1)} all-to-all(bf16[4,4,32,768]{3,2,1,0:T(8,128)(2,1)S(1)} %broadcast_in_dim.66), channel_id=1, replica_groups=mesh['x'=4,'h'=4,'m'=2,'p'=2,'y'=4,'c'=2] {'y'}, dimensions={0} | all-to-all | bytes 1572864 | tf_op jit(solution)/shard_map/all_to_all | solution.py:16
  18.3 1.9 %collective-permute-start = (bf16[512,768]{1,0:T(8,128)(2,1)S(1)}, bf16[512,768]{1,0:T(8,128)(2,1)S(1)}, u32[]{:S(2)}, u32[]{:S(2)}) collective-permute-start(bf16[512,768]{1,0:T(8,128)(2,1)S(1)} %bitcast.69), channel_id=1, source_target_pairs={{0,1},{1,0},{2,3},{3,2},{4,5},{5,4},{6,7},{7,6},{8,9},{9,8},{10,11... | collective-permute-start | bytes 2359304 | tf_op jit(solution)/shard_map/ppermute | solution.py:27
  20.3 1.0 multiply_reduce_fusion.1
  21.3 0.4 exponential_reduce_fusion.1
  21.6 0.8 collective-permute-done
  22.5 1.0 multiply_reduce_fusion
  23.5 0.4 exponential_reduce_fusion
  24.0 28.1 %all_to_all.31 = f32[16,8,128]{2,1,0:T(8,128)S(1)} all-to-all(f32[16,8,128]{2,1,0:T(8,128)S(1)} %bitcast.78), channel_id=1, replica_groups=mesh['x'=4,'h'=4,'m'=2,'p'=2,'y'=4,'c'=2] {'h','m','p'}, dimensions={0} | all-to-all | bytes 131072 | tf_op jit(solution)/shard_map/all_to_all | solution.py:23
  52.1 0.7 broadcast_in_dim.68
  52.9 6.5 %all-to-all-start.2 = ((f32[64,8,128]{2,1,0:T(8,128)}), f32[64,8,128]{2,1,0:T(8,128)S(1)}, u32[]{:S(2)}, u32[]{:S(2)}) async-start(f32[64,8,128]{2,1,0:T(8,128)} %broadcast_in_dim.68), calls=%async_computation.2 | async-start | bytes 524288 | tf_op jit(solution)/shard_map/all_to_all | solution.py:16
  59.4 7.9 %all-to-all-done.2 = f32[64,8,128]{2,1,0:T(8,128)S(1)} async-done(((f32[64,8,128]{2,1,0:T(8,128)}), f32[64,8,128]{2,1,0:T(8,128)S(1)}, u32[]{:S(2)}, u32[]{:S(2)}) %all-to-all-start.2) | async-done | bytes 262176 | tf_op jit(solution)/shard_map/all_to_all | solution.py:16
  67.4 0.1 reshape.123
  67.6 0.1 reshape.122
  67.8 0.1 reduce_sum.109
  68.4 1.1 multiply_convert_fusion
  69.6 1.9 %bitcast_convert_fusion = bf16[512,768]{1,0:T(8,128)(2,1)} fusion(bf16[512,2,512]{0,2,1:T(8,128)(2,1)S(1)} %multiply_convert_fusion, bf16[2,512,768]{2,1,0:T(8,128)(2,1)S(1)} %copy-done), kind=kOutput, calls=%fused_computation.7 | convolution fusion | flops 805699584 | bytes 3407872 | tf_op jit(solution)/shard_map/dot_general | solution.py:102
  71.5 1.9 %collective-permute-start.1 = (bf16[512,768]{1,0:T(8,128)(2,1)}, bf16[512,768]{1,0:T(8,128)(2,1)S(1)}, u32[]{:S(2)}, u32[]{:S(2)}) collective-permute-start(bf16[512,768]{1,0:T(8,128)(2,1)} %bitcast_convert_fusion), channel_id=1, source_target_pairs={{0,1},{1,0},{2,3},{3,2},{4,5},{5,4},{6,7},{7,6},{8,9},{9,8},{10,11... | collective-permute-start | bytes 2359304 | tf_op jit(solution)/shard_map/ppermute | solution.py:27
  73.6 1.1 multiply_convert_fusion.1
  74.7 1.0 convolution_bitcast_fusion
  75.8 0.1 collective-permute-done.1
  75.9 0.2 add_convert_fusion.1
  76.1 18.5 %all_to_all.32 = bf16[32,16,768]{2,1,0:T(8,128)(2,1)S(1)} all-to-all(bf16[32,16,768]{2,1,0:T(8,128)(2,1)S(1)} %bitcast.73), channel_id=1, replica_groups=mesh['x'=4,'h'=4,'m'=2,'p'=2,'y'=4,'c'=2] {'y','x','p'}, dimensions={0} | all-to-all | bytes 1572864 | tf_op jit(solution)/shard_map/all_to_all | solution.py:37
  94.6 0.1 reduce_sum.113
  94.7 17.7 %all_to_all.33 = bf16[8,8,768]{2,1,0:T(8,128)(2,1)S(1)} all-to-all(bf16[8,8,768]{2,1,0:T(8,128)(2,1)S(1)} %bitcast.77), channel_id=1, replica_groups=mesh['x'=4,'h'=4,'m'=2,'p'=2,'y'=4,'c'=2] {'h','m'}, dimensions={0} | all-to-all | bytes 196608 | tf_op jit(solution)/shard_map/all_to_all | solution.py:23
  112.4 0.7 broadcast_in_dim.78
  113.1 5.6 %all-to-all-start.5 = ((bf16[16,8,768]{2,1,0:T(8,128)(2,1)}), bf16[16,8,768]{2,1,0:T(8,128)(2,1)S(1)}, u32[]{:S(2)}, u32[]{:S(2)}) async-start(bf16[16,8,768]{2,1,0:T(8,128)(2,1)} %broadcast_in_dim.78), calls=%async_computation.5 | async-start | bytes 393216 | tf_op jit(solution)/shard_map/all_to_all | solution.py:16
  118.7 2.3 %fusion.12 = f32[2,512,768]{2,1,0:T(8,128)S(1)} fusion(bf16[512,2,512]{0,2,1:T(8,128)(2,1)} %copy-done.3, bf16[512,768,1]{1,0,2:T(8,128)(2,1)S(1)} %bitcast.72), kind=kOutput, calls=%fused_computation.43 | convolution fusion | flops 805306368 | bytes 4980736 | tf_op jit(solution)/shard_map/dot_general | solution.py:117
  121.1 2.1 %add_convert_fusion = bf16[2,512,768]{2,1,0:T(8,128)(2,1)} fusion(f32[2,512,768]{2,1,0:T(8,128)S(1)} %fusion.12, bf16[512,2,512]{0,2,1:T(8,128)(2,1)S(1)} %copy-done.2, bf16[512,768]{1,0:T(8,128)(2,1)S(1)} %copy-done.5), kind=kOutput, calls=%fused_computation | convolution fusion | flops 806879232 | bytes 6553600 | tf_op jit(solution)/shard_map/dot_general | solution.py:117
  123.2 0.6 subtract_reduce_fusion
  124.5 0.9 all-to-all-done.5
  125.4 0.7 copy.33
  (50 shorter events, 1.0 us)
Async XLA Ops:
  0.6 19.6 %copy-start = (bf16[2,512,768]{2,1,0:T(8,128)(2,1)S(1)}, bf16[2,512,768]{2,1,0:T(8,128)(2,1)}, u32[]{:S(2)}) copy-start(bf16[2,512,768]{2,1,0:T(8,128)(2,1)} %param.4) | copy-start | bytes 4718596
  18.3 4.2 %collective-permute-start = (bf16[512,768]{1,0:T(8,128)(2,1)S(1)}, bf16[512,768]{1,0:T(8,128)(2,1)S(1)}, u32[]{:S(2)}, u32[]{:S(2)}) collective-permute-start(bf16[512,768]{1,0:T(8,128)(2,1)S(1)} %bitcast.69), channel_id=1, source_target_pairs={{0,1},{1,0},{2,3},{3,2},{4,5},{5,4},{6,7},{7,6},{8,9},{9,8},{10,11... | collective-permute-start | bytes 2359304 | tf_op jit(solution)/shard_map/ppermute | solution.py:27
  22.5 46.0 %copy-start.4 = (bf16[512,768]{1,0:T(8,128)(2,1)}, bf16[512,768]{1,0:T(8,128)(2,1)S(1)}, u32[]{:S(2)}) copy-start(bf16[512,768]{1,0:T(8,128)(2,1)S(1)} %collective-permute-done) | copy-start | bytes 2359300
  23.5 44.1 %copy-start.6 = (s32[32,4]{0,1:T(4,128)S(1)}, s32[32,4]{0,1:T(4,128)}, u32[]{:S(2)}) copy-start(s32[32,4]{0,1:T(4,128)} %param.5) | copy-start | bytes 1540
  52.9 14.5 %all-to-all-start.2 = ((f32[64,8,128]{2,1,0:T(8,128)}), f32[64,8,128]{2,1,0:T(8,128)S(1)}, u32[]{:S(2)}, u32[]{:S(2)}) async-start(f32[64,8,128]{2,1,0:T(8,128)} %broadcast_in_dim.68), calls=%async_computation.2 | async-start | bytes 524288 | tf_op jit(solution)/shard_map/all_to_all | solution.py:16
  69.6 1.9 %copy-start.1 = (bf16[512,2,512]{0,2,1:T(8,128)(2,1)}, bf16[512,2,512]{0,2,1:T(8,128)(2,1)S(1)}, u32[]{:S(2)}) copy-start(bf16[512,2,512]{0,2,1:T(8,128)(2,1)S(1)} %multiply_convert_fusion) | copy-start | bytes 3145732
  71.5 4.4 %collective-permute-start.1 = (bf16[512,768]{1,0:T(8,128)(2,1)}, bf16[512,768]{1,0:T(8,128)(2,1)S(1)}, u32[]{:S(2)}, u32[]{:S(2)}) collective-permute-start(bf16[512,768]{1,0:T(8,128)(2,1)} %bitcast_convert_fusion), channel_id=1, source_target_pairs={{0,1},{1,0},{2,3},{3,2},{4,5},{5,4},{6,7},{7,6},{8,9},{9,8},{10,11... | collective-permute-start | bytes 2359304 | tf_op jit(solution)/shard_map/ppermute | solution.py:27
  74.7 1.1 copy-start.3
  113.1 12.2 %all-to-all-start.5 = ((bf16[16,8,768]{2,1,0:T(8,128)(2,1)}), bf16[16,8,768]{2,1,0:T(8,128)(2,1)S(1)}, u32[]{:S(2)}, u32[]{:S(2)}) async-start(bf16[16,8,768]{2,1,0:T(8,128)(2,1)} %broadcast_in_dim.78), calls=%async_computation.5 | async-start | bytes 393216 | tf_op jit(solution)/shard_map/all_to_all | solution.py:16
  118.7 2.4 %copy-start.2 = (bf16[512,2,512]{0,2,1:T(8,128)(2,1)S(1)}, bf16[512,2,512]{0,2,1:T(8,128)(2,1)}, u32[]{:S(2)}) copy-start(bf16[512,2,512]{0,2,1:T(8,128)(2,1)} %copy-done.1) | copy-start | bytes 3145732
  118.7 2.4 %copy-start.5 = (bf16[512,768]{1,0:T(8,128)(2,1)S(1)}, bf16[512,768]{1,0:T(8,128)(2,1)}, u32[]{:S(2)}) copy-start(bf16[512,768]{1,0:T(8,128)(2,1)} %copy-done.4) | copy-start | bytes 2359300

commit v6 on v5

--- a/solution.py
+++ b/solution.py
@@ -65,28 +65,30 @@
 
     own_order = jnp.concatenate(local_lse).T.reshape(local_docs, 2, -1, 128)
     lse = jnp.where(core == 0, own_order, own_order[:, ::-1]).reshape(-1, 128)
+    group = lax.axis_index(QG)
+    by_core = candidates.reshape(rows_of_y, 2, per_group, slots).swapaxes(0, 1)
+    by_core = by_core.reshape(total_queries, slots)
+    place = (group * local_docs, group * own_order.size // 128, core, by_core)
+    lse, place = lax.optimization_barrier((lse, place))
     lse = log_of_sum(shared_and_scattered(lse, ("h", "m"), "p"))
     everyone = copy_for_each(lse, ("x", *QG, "p"))
+    everyone, place = lax.optimization_barrier((everyone, place))
+    first_doc, first_row, core, by_core = place
     lse = log_of_sum(everyone.reshape(lax.axis_size("x"), -1, 128))
-    lse, candidates, core, group = lax.optimization_barrier(
-        (lse, candidates, core, lax.axis_index(QG))
-    )
 
     all_docs = groups * local_docs
     scores = jnp.sum(lse.reshape(all_docs, total_queries, query_len), axis=2) / sharpness_factor
-    by_core = candidates.reshape(rows_of_y, 2, per_group, slots).swapaxes(0, 1)
-    by_core = by_core.reshape(total_queries, slots)
     picks = by_core[:, :, None] == jnp.arange(all_docs, dtype=jnp.int32)[None, None, :]
     pair = jnp.sum(jnp.where(picks, scores.T[:, None, :], 0.0), axis=2)
     highest = jnp.max(pair, axis=1, keepdims=True)
     total = highest + jnp.log(jnp.sum(jnp.exp(pair - highest), axis=1, keepdims=True))
-    first = lax.broadcasted_iota(jnp.int32, pair.shape, 1) == 0
+    first = lax.broadcasted_iota(jnp.int32, pair.shape, 1) == jnp.minimum(first_doc, 0)
     dz = loss_scale / total_queries * (jnp.exp(pair - total) - jnp.where(first, 1.0, 0.0))
-    owned = by_core[:, :, None] - group * local_docs == jnp.arange(local_docs, dtype=jnp.int32)
+    owned = by_core[:, :, None] - first_doc == jnp.arange(local_docs, dtype=jnp.int32)
     weights = jnp.sum(jnp.where(owned, dz[:, :, None], 0.0), axis=1).reshape(2, -1, local_docs)
     weights = jnp.where(core == 0, weights, weights[::-1]).reshape(total_queries, local_docs)
     row_weight = jnp.repeat(weights, query_len, axis=0)
-    mine = lax.dynamic_slice_in_dim(lse, group * len(own_order.reshape(-1, 128)), len(lse) // groups)
+    mine = lax.dynamic_slice_in_dim(lse, first_row, own_order.size // 128)
     mine = mine.reshape(own_order.shape)
     norm = jnp.where(core == 0, mine, mine[:, ::-1]).reshape(local_docs, -1).T
 

time: 128 us -> 127 us (level)
  blocking collectives: 80.8 us -> 95.1 us
  waiting for transfers between devices: 9.76 us -> 1.65 us
  starting transfers between devices: 15.9 us -> 9.4 us
    all_to_all x1 -> x2, blocking collectives: 16.6 us -> 30.8 us  [copy_for_each(): return lax.all_to_all(copies, axis, split_axis=0, concat_axis=0, tiled=True)]
    all_to_all x2 -> x1, waiting for transfers between devices: 8.81 us -> 0.9 us  [copy_for_each(): return lax.all_to_all(copies, axis, split_axis=0, concat_axis=0, tiled=True)]
    all_to_all x2 -> x1, starting transfers between devices: 12.1 us -> 5.59 us  [copy_for_each(): return lax.all_to_all(copies, axis, split_axis=0, concat_axis=0, tiled=True)]
  transfers between devices with their start and end apart: 4 -> 3, of which waited for: 4 -> 3; matrix products, arithmetic and copies ran while one was open for 7% -> 7% of each run, Pallas kernels for 0% -> 0%
where the time goes in v6:
time: 127 us; the launch traced here: 126 us
  blocking collectives  95.1 us (75%)
  matrix products  11.7 us (9%)
  starting transfers between devices  9.4 us (7%)
  local copies, waits for them, and re-layouts  3.34 us (3%)
  between operations  2.71 us (2%)
  other arithmetic  2.17 us (2%)
  waiting for transfers between devices  1.65 us (1%)
    all_to_all x2, blocking collectives, shared_and_scattered(): lax.all_to_all(copies, (*far, near), split_axis=0, concat_axis=0, tiled=T...  45.8 us
    all_to_all x2, blocking collectives, copy_for_each(): return lax.all_to_all(copies, axis, split_axis=0, concat_axis=0, tiled=True)  30.8 us
    all_to_all x1, blocking collectives, sent_and_summed(): lax.all_to_all(tiles, axis, split_axis=0, concat_axis=0, tiled=True)  18.5 us
    all_to_all x1, starting transfers between devices, copy_for_each(): return lax.all_to_all(copies, axis, split_axis=0, concat_axis=0, tiled=True)  5.59 us
    dot_general x2, matrix products, per_device(): lax.dot_general(w, rows, (((0,), (0,)), ((), ())), preferred_element_type...  4.46 us
    dot_general x4, matrix products, scored(): lax.dot_general(rows, documents, (((1,), (2,)), ((), ())), preferred_elem...  4.3 us
    ppermute x2, starting transfers between devices, other_core(): return lax.ppermute(x, 'c', [(0, 1), (1, 0)])  3.82 us
    dot_general x2, matrix products, grad_of_rows(): lax.dot_general(weighted, documents, (((1, 2), (0, 1)), ((), ())), prefer...  2.95 us
  transfers between devices with their start and end apart: 3, of which 3 were waited for; matrix products, arithmetic and copies ran while one was open for 7% of the time, Pallas kernels for 0%

profile of v6, /device:TPU:6, one launch (start us, length us, event | category | flops | bytes accessed | tf_op | source)
XLA Modules:
  0.0 126.1 jit_solution(5522901925405160460)
XLA Ops:
  0.7 1.1 broadcast_in_dim.68
  1.8 16.6 %all_to_all.30 = bf16[4,4,32,768]{3,2,1,0:T(8,128)(2,1)S(1)} all-to-all(bf16[4,4,32,768]{3,2,1,0:T(8,128)(2,1)S(1)} %broadcast_in_dim.68), channel_id=1, replica_groups=mesh['x'=4,'h'=4,'m'=2,'p'=2,'y'=4,'c'=2] {'y'}, dimensions={0} | all-to-all | bytes 1572864 | tf_op jit(solution)/shard_map/all_to_all | solution.py:16
  18.3 1.9 %collective-permute-start = (bf16[512,768]{1,0:T(8,128)(2,1)S(1)}, bf16[512,768]{1,0:T(8,128)(2,1)S(1)}, u32[]{:S(2)}, u32[]{:S(2)}) collective-permute-start(bf16[512,768]{1,0:T(8,128)(2,1)S(1)} %bitcast.70), channel_id=1, source_target_pairs={{0,1},{1,0},{2,3},{3,2},{4,5},{5,4},{6,7},{7,6},{8,9},{9,8},{10,11... | collective-permute-start | bytes 2359304 | tf_op jit(solution)/shard_map/ppermute | solution.py:27
  20.3 0.1 reshape.125
  20.4 0.1 reshape.126
  20.5 1.0 multiply_reduce_fusion.1
  21.5 0.4 exponential_reduce_fusion.1
  21.9 0.6 collective-permute-done
  22.5 1.0 multiply_reduce_fusion
  23.5 0.4 exponential_reduce_fusion
  24.0 28.1 %all_to_all.31 = f32[16,8,128]{2,1,0:T(8,128)S(1)} all-to-all(f32[16,8,128]{2,1,0:T(8,128)S(1)} %bitcast.79), channel_id=1, replica_groups=mesh['x'=4,'h'=4,'m'=2,'p'=2,'y'=4,'c'=2] {'h','m','p'}, dimensions={0} | all-to-all | bytes 131072 | tf_op jit(solution)/shard_map/all_to_all | solution.py:23
  52.2 14.2 %all_to_all.32 = f32[64,8,128]{2,1,0:T(8,128)S(1)} all-to-all(f32[64,8,128]{2,1,0:T(8,128)S(1)} %broadcast_in_dim.70), channel_id=1, replica_groups=mesh['x'=4,'h'=4,'m'=2,'p'=2,'y'=4,'c'=2] {'x','y','c','p'}, dimensions={0} | all-to-all | bytes 524288 | tf_op jit(solution)/shard_map/all_to_all | solution.py:16
  66.5 0.1 add.50
  66.7 0.1 reduce_sum.109
  67.2 0.1 slice.36
  67.3 1.1 multiply_convert_fusion
  68.5 1.9 %bitcast_convert_fusion = bf16[512,768]{1,0:T(8,128)(2,1)} fusion(bf16[512,2,512]{0,2,1:T(8,128)(2,1)S(1)} %multiply_convert_fusion, bf16[2,512,768]{2,1,0:T(8,128)(2,1)S(1)} %copy-done), kind=kOutput, calls=%fused_computation.7 | convolution fusion | flops 805699584 | bytes 3407872 | tf_op jit(solution)/shard_map/dot_general | solution.py:104
  70.4 1.9 %collective-permute-start.1 = (bf16[512,768]{1,0:T(8,128)(2,1)}, bf16[512,768]{1,0:T(8,128)(2,1)S(1)}, u32[]{:S(2)}, u32[]{:S(2)}) collective-permute-start(bf16[512,768]{1,0:T(8,128)(2,1)} %bitcast_convert_fusion), channel_id=1, source_target_pairs={{0,1},{1,0},{2,3},{3,2},{4,5},{5,4},{6,7},{7,6},{8,9},{9,8},{10,11... | collective-permute-start | bytes 2359304 | tf_op jit(solution)/shard_map/ppermute | solution.py:27
  72.5 1.1 multiply_convert_fusion.1
  73.6 1.0 convolution_bitcast_fusion
  74.7 0.1 collective-permute-done.1
  74.8 0.2 add_convert_fusion.1
  75.0 18.5 %all_to_all.33 = bf16[32,16,768]{2,1,0:T(8,128)(2,1)S(1)} all-to-all(bf16[32,16,768]{2,1,0:T(8,128)(2,1)S(1)} %bitcast.74), channel_id=1, replica_groups=mesh['x'=4,'h'=4,'m'=2,'p'=2,'y'=4,'c'=2] {'y','x','p'}, dimensions={0} | all-to-all | bytes 1572864 | tf_op jit(solution)/shard_map/all_to_all | solution.py:37
  93.5 0.1 reduce_sum.113
  93.6 17.7 %all_to_all.34 = bf16[8,8,768]{2,1,0:T(8,128)(2,1)S(1)} all-to-all(bf16[8,8,768]{2,1,0:T(8,128)(2,1)S(1)} %bitcast.78), channel_id=1, replica_groups=mesh['x'=4,'h'=4,'m'=2,'p'=2,'y'=4,'c'=2] {'h','m'}, dimensions={0} | all-to-all | bytes 196608 | tf_op jit(solution)/shard_map/all_to_all | solution.py:23
  111.3 0.7 broadcast_in_dim.80
  112.0 5.6 %all-to-all-start.5 = ((bf16[16,8,768]{2,1,0:T(8,128)(2,1)}), bf16[16,8,768]{2,1,0:T(8,128)(2,1)S(1)}, u32[]{:S(2)}, u32[]{:S(2)}) async-start(bf16[16,8,768]{2,1,0:T(8,128)(2,1)} %broadcast_in_dim.80), calls=%async_computation.5 | async-start | bytes 393216 | tf_op jit(solution)/shard_map/all_to_all | solution.py:16
  117.6 2.3 %fusion.12 = f32[2,512,768]{2,1,0:T(8,128)S(1)} fusion(bf16[512,2,512]{0,2,1:T(8,128)(2,1)} %copy-done.3, bf16[512,768,1]{1,0,2:T(8,128)(2,1)S(1)} %bitcast.73), kind=kOutput, calls=%fused_computation.43 | convolution fusion | flops 805306368 | bytes 4980736 | tf_op jit(solution)/shard_map/dot_general | solution.py:119
  120.0 2.1 %add_convert_fusion = bf16[2,512,768]{2,1,0:T(8,128)(2,1)} fusion(f32[2,512,768]{2,1,0:T(8,128)S(1)} %fusion.12, bf16[512,2,512]{0,2,1:T(8,128)(2,1)S(1)} %copy-done.2, bf16[512,768]{1,0:T(8,128)(2,1)S(1)} %copy-done.5), kind=kOutput, calls=%fused_computation | convolution fusion | flops 806879232 | bytes 6553600 | tf_op jit(solution)/shard_map/dot_general | solution.py:119
  122.1 0.6 subtract_reduce_fusion
  123.4 0.9 all-to-all-done.5
  124.3 0.7 copy.33
  (49 shorter events, 0.9 us)
Async XLA Ops:
  0.6 19.8 %copy-start = (bf16[2,512,768]{2,1,0:T(8,128)(2,1)S(1)}, bf16[2,512,768]{2,1,0:T(8,128)(2,1)}, u32[]{:S(2)}) copy-start(bf16[2,512,768]{2,1,0:T(8,128)(2,1)} %param.4) | copy-start | bytes 4718596
  0.6 19.6 %copy-start.6 = (s32[32,4]{0,1:T(4,128)S(1)}, s32[32,4]{0,1:T(4,128)}, u32[]{:S(2)}) copy-start(s32[32,4]{0,1:T(4,128)} %param.5) | copy-start | bytes 1540
  18.3 4.2 %collective-permute-start = (bf16[512,768]{1,0:T(8,128)(2,1)S(1)}, bf16[512,768]{1,0:T(8,128)(2,1)S(1)}, u32[]{:S(2)}, u32[]{:S(2)}) collective-permute-start(bf16[512,768]{1,0:T(8,128)(2,1)S(1)} %bitcast.70), channel_id=1, source_target_pairs={{0,1},{1,0},{2,3},{3,2},{4,5},{5,4},{6,7},{7,6},{8,9},{9,8},{10,11... | collective-permute-start | bytes 2359304 | tf_op jit(solution)/shard_map/ppermute | solution.py:27
  22.5 44.8 %copy-start.4 = (bf16[512,768]{1,0:T(8,128)(2,1)}, bf16[512,768]{1,0:T(8,128)(2,1)S(1)}, u32[]{:S(2)}) copy-start(bf16[512,768]{1,0:T(8,128)(2,1)S(1)} %collective-permute-done) | copy-start | bytes 2359300
  68.5 1.9 %copy-start.1 = (bf16[512,2,512]{0,2,1:T(8,128)(2,1)}, bf16[512,2,512]{0,2,1:T(8,128)(2,1)S(1)}, u32[]{:S(2)}) copy-start(bf16[512,2,512]{0,2,1:T(8,128)(2,1)S(1)} %multiply_convert_fusion) | copy-start | bytes 3145732
  70.4 4.4 %collective-permute-start.1 = (bf16[512,768]{1,0:T(8,128)(2,1)}, bf16[512,768]{1,0:T(8,128)(2,1)S(1)}, u32[]{:S(2)}, u32[]{:S(2)}) collective-permute-start(bf16[512,768]{1,0:T(8,128)(2,1)} %bitcast_convert_fusion), channel_id=1, source_target_pairs={{0,1},{1,0},{2,3},{3,2},{4,5},{5,4},{6,7},{7,6},{8,9},{9,8},{10,11... | collective-permute-start | bytes 2359304 | tf_op jit(solution)/shard_map/ppermute | solution.py:27
  73.6 1.1 copy-start.3
  112.0 12.2 %all-to-all-start.5 = ((bf16[16,8,768]{2,1,0:T(8,128)(2,1)}), bf16[16,8,768]{2,1,0:T(8,128)(2,1)S(1)}, u32[]{:S(2)}, u32[]{:S(2)}) async-start(bf16[16,8,768]{2,1,0:T(8,128)(2,1)} %broadcast_in_dim.80), calls=%async_computation.5 | async-start | bytes 393216 | tf_op jit(solution)/shard_map/all_to_all | solution.py:16
  117.6 2.4 %copy-start.2 = (bf16[512,2,512]{0,2,1:T(8,128)(2,1)S(1)}, bf16[512,2,512]{0,2,1:T(8,128)(2,1)}, u32[]{:S(2)}) copy-start(bf16[512,2,512]{0,2,1:T(8,128)(2,1)} %copy-done.1) | copy-start | bytes 3145732
  117.6 2.4 %copy-start.5 = (bf16[512,768]{1,0:T(8,128)(2,1)S(1)}, bf16[512,768]{1,0:T(8,128)(2,1)}, u32[]{:S(2)}) copy-start(bf16[512,768]{1,0:T(8,128)(2,1)} %copy-done.4) | copy-start | bytes 2359300

commit v7 on v6

--- a/solution.py
+++ b/solution.py
@@ -71,10 +71,10 @@
     place = (group * local_docs, group * own_order.size // 128, core, by_core)
     lse, place = lax.optimization_barrier((lse, place))
     lse = log_of_sum(shared_and_scattered(lse, ("h", "m"), "p"))
-    everyone = copy_for_each(lse, ("x", *QG, "p"))
+    everyone = copy_for_each(lse, (*QG, "x", "p"))
     everyone, place = lax.optimization_barrier((everyone, place))
     first_doc, first_row, core, by_core = place
-    lse = log_of_sum(everyone.reshape(lax.axis_size("x"), -1, 128))
+    lse = log_of_sum(everyone.reshape(groups, lax.axis_size("x"), -1, 128).swapaxes(0, 1)).reshape(-1, 128)
 
     all_docs = groups * local_docs
     scores = jnp.sum(lse.reshape(all_docs, total_queries, query_len), axis=2) / sharpness_factor

time: 127 us -> 127 us (level)
  no operation moved by 1% of the time
where the time goes in v7:
time: 127 us; the launch traced here: 126 us
  blocking collectives  94.8 us (75%)
  matrix products  11.7 us (9%)
  starting transfers between devices  9.4 us (7%)
  local copies, waits for them, and re-layouts  3.34 us (3%)
  between operations  2.72 us (2%)
  other arithmetic  2.18 us (2%)
  waiting for transfers between devices  1.65 us (1%)
    all_to_all x2, blocking collectives, shared_and_scattered(): lax.all_to_all(copies, (*far, near), split_axis=0, concat_axis=0, tiled=T...  45.8 us
    all_to_all x2, blocking collectives, copy_for_each(): return lax.all_to_all(copies, axis, split_axis=0, concat_axis=0, tiled=True)  31 us
    all_to_all x1, blocking collectives, sent_and_summed(): lax.all_to_all(tiles, axis, split_axis=0, concat_axis=0, tiled=True)  18 us
    all_to_all x1, starting transfers between devices, copy_for_each(): return lax.all_to_all(copies, axis, split_axis=0, concat_axis=0, tiled=True)  5.59 us
    dot_general x2, matrix products, per_device(): lax.dot_general(w, rows, (((0,), (0,)), ((), ())), preferred_element_type...  4.46 us
    dot_general x4, matrix products, scored(): lax.dot_general(rows, documents, (((1,), (2,)), ((), ())), preferred_elem...  4.29 us
    ppermute x2, starting transfers between devices, other_core(): return lax.ppermute(x, 'c', [(0, 1), (1, 0)])  3.82 us
    dot_general x2, matrix products, grad_of_rows(): lax.dot_general(weighted, documents, (((1, 2), (0, 1)), ((), ())), prefer...  2.95 us
  transfers between devices with their start and end apart: 3, of which 3 were waited for; matrix products, arithmetic and copies ran while one was open for 7% of the time, Pallas kernels for 0%

profile of v7, /device:TPU:6, one launch (start us, length us, event | category | flops | bytes accessed | tf_op | source)
XLA Modules:
  0.0 125.8 jit_solution(14244296199335820089)
XLA Ops:
  0.7 1.1 broadcast_in_dim.68
  1.8 16.6 %all_to_all.30 = bf16[4,4,32,768]{3,2,1,0:T(8,128)(2,1)S(1)} all-to-all(bf16[4,4,32,768]{3,2,1,0:T(8,128)(2,1)S(1)} %broadcast_in_dim.68), channel_id=1, replica_groups=mesh['x'=4,'h'=4,'m'=2,'p'=2,'y'=4,'c'=2] {'y'}, dimensions={0} | all-to-all | bytes 1572864 | tf_op jit(solution)/shard_map/all_to_all | solution.py:16
  18.3 1.9 %collective-permute-start = (bf16[512,768]{1,0:T(8,128)(2,1)S(1)}, bf16[512,768]{1,0:T(8,128)(2,1)S(1)}, u32[]{:S(2)}, u32[]{:S(2)}) collective-permute-start(bf16[512,768]{1,0:T(8,128)(2,1)S(1)} %bitcast.65), channel_id=1, source_target_pairs={{0,1},{1,0},{2,3},{3,2},{4,5},{5,4},{6,7},{7,6},{8,9},{9,8},{10,11... | collective-permute-start | bytes 2359304 | tf_op jit(solution)/shard_map/ppermute | solution.py:27
  20.3 0.1 reshape.129
  20.4 0.1 reshape.130
  20.5 1.0 multiply_reduce_fusion.1
  21.5 0.4 exponential_reduce_fusion.1
  21.9 0.6 collective-permute-done
  22.5 1.0 multiply_reduce_fusion
  23.5 0.4 exponential_reduce_fusion
  24.0 28.1 %all_to_all.31 = f32[16,8,128]{2,1,0:T(8,128)S(1)} all-to-all(f32[16,8,128]{2,1,0:T(8,128)S(1)} %bitcast.75), channel_id=1, replica_groups=mesh['x'=4,'h'=4,'m'=2,'p'=2,'y'=4,'c'=2] {'h','m','p'}, dimensions={0} | all-to-all | bytes 131072 | tf_op jit(solution)/shard_map/all_to_all | solution.py:23
  52.2 14.4 %all_to_all.32 = f32[64,8,128]{2,1,0:T(8,128)S(1)} all-to-all(f32[64,8,128]{2,1,0:T(8,128)S(1)} %broadcast_in_dim.70), channel_id=1, replica_groups=mesh['x'=4,'h'=4,'m'=2,'p'=2,'y'=4,'c'=2] {'y','c','x','p'}, dimensions={0} | all-to-all | bytes 524288 | tf_op jit(solution)/shard_map/all_to_all | solution.py:16
  66.7 0.1 add.55
  66.9 0.1 reduce_sum.109
  67.4 0.1 slice.36
  67.5 1.1 multiply_convert_fusion
  68.7 1.9 %bitcast_convert_fusion = bf16[512,768]{1,0:T(8,128)(2,1)} fusion(bf16[512,2,512]{0,2,1:T(8,128)(2,1)S(1)} %multiply_convert_fusion, bf16[2,512,768]{2,1,0:T(8,128)(2,1)S(1)} %copy-done), kind=kOutput, calls=%fused_computation.7 | convolution fusion | flops 805699584 | bytes 3407872 | tf_op jit(solution)/shard_map/dot_general | solution.py:104
  70.6 1.9 %collective-permute-start.1 = (bf16[512,768]{1,0:T(8,128)(2,1)}, bf16[512,768]{1,0:T(8,128)(2,1)S(1)}, u32[]{:S(2)}, u32[]{:S(2)}) collective-permute-start(bf16[512,768]{1,0:T(8,128)(2,1)} %bitcast_convert_fusion), channel_id=1, source_target_pairs={{0,1},{1,0},{2,3},{3,2},{4,5},{5,4},{6,7},{7,6},{8,9},{9,8},{10,11... | collective-permute-start | bytes 2359304 | tf_op jit(solution)/shard_map/ppermute | solution.py:27
  72.7 1.1 multiply_convert_fusion.1
  73.8 1.0 convolution_bitcast_fusion
  74.9 0.1 collective-permute-done.1
  75.0 0.2 add_convert_fusion.1
  75.2 18.0 %all_to_all.33 = bf16[32,16,768]{2,1,0:T(8,128)(2,1)S(1)} all-to-all(bf16[32,16,768]{2,1,0:T(8,128)(2,1)S(1)} %bitcast.69), channel_id=1, replica_groups=mesh['x'=4,'h'=4,'m'=2,'p'=2,'y'=4,'c'=2] {'y','x','p'}, dimensions={0} | all-to-all | bytes 1572864 | tf_op jit(solution)/shard_map/all_to_all | solution.py:37
  93.2 0.1 reduce_sum.113
  93.4 17.7 %all_to_all.34 = bf16[8,8,768]{2,1,0:T(8,128)(2,1)S(1)} all-to-all(bf16[8,8,768]{2,1,0:T(8,128)(2,1)S(1)} %bitcast.73), channel_id=1, replica_groups=mesh['x'=4,'h'=4,'m'=2,'p'=2,'y'=4,'c'=2] {'h','m'}, dimensions={0} | all-to-all | bytes 196608 | tf_op jit(solution)/shard_map/all_to_all | solution.py:23
  111.1 0.7 broadcast_in_dim.80
  111.8 5.6 %all-to-all-start.5 = ((bf16[16,8,768]{2,1,0:T(8,128)(2,1)}), bf16[16,8,768]{2,1,0:T(8,128)(2,1)S(1)}, u32[]{:S(2)}, u32[]{:S(2)}) async-start(bf16[16,8,768]{2,1,0:T(8,128)(2,1)} %broadcast_in_dim.80), calls=%async_computation.5 | async-start | bytes 393216 | tf_op jit(solution)/shard_map/all_to_all | solution.py:16
  117.4 2.3 %fusion.10 = f32[2,512,768]{2,1,0:T(8,128)S(1)} fusion(bf16[512,2,512]{0,2,1:T(8,128)(2,1)} %copy-done.3, bf16[512,768,1]{1,0,2:T(8,128)(2,1)S(1)} %bitcast.68), kind=kOutput, calls=%fused_computation.40 | convolution fusion | flops 805306368 | bytes 4980736 | tf_op jit(solution)/shard_map/dot_general | solution.py:119
  119.7 2.1 %add_convert_fusion = bf16[2,512,768]{2,1,0:T(8,128)(2,1)} fusion(f32[2,512,768]{2,1,0:T(8,128)S(1)} %fusion.10, bf16[512,2,512]{0,2,1:T(8,128)(2,1)S(1)} %copy-done.2, bf16[512,768]{1,0:T(8,128)(2,1)S(1)} %copy-done.5), kind=kOutput, calls=%fused_computation | convolution fusion | flops 806879232 | bytes 6553600 | tf_op jit(solution)/shard_map/dot_general | solution.py:119
  121.8 0.6 subtract_reduce_fusion
  123.1 0.9 all-to-all-done.5
  124.0 0.7 copy.33
  (49 shorter events, 0.9 us)
Async XLA Ops:
  0.6 19.8 %copy-start = (bf16[2,512,768]{2,1,0:T(8,128)(2,1)S(1)}, bf16[2,512,768]{2,1,0:T(8,128)(2,1)}, u32[]{:S(2)}) copy-start(bf16[2,512,768]{2,1,0:T(8,128)(2,1)} %param.4) | copy-start | bytes 4718596
  0.6 19.6 %copy-start.6 = (s32[32,4]{0,1:T(4,128)S(1)}, s32[32,4]{0,1:T(4,128)}, u32[]{:S(2)}) copy-start(s32[32,4]{0,1:T(4,128)} %param.5) | copy-start | bytes 1540
  18.3 4.2 %collective-permute-start = (bf16[512,768]{1,0:T(8,128)(2,1)S(1)}, bf16[512,768]{1,0:T(8,128)(2,1)S(1)}, u32[]{:S(2)}, u32[]{:S(2)}) collective-permute-start(bf16[512,768]{1,0:T(8,128)(2,1)S(1)} %bitcast.65), channel_id=1, source_target_pairs={{0,1},{1,0},{2,3},{3,2},{4,5},{5,4},{6,7},{7,6},{8,9},{9,8},{10,11... | collective-permute-start | bytes 2359304 | tf_op jit(solution)/shard_map/ppermute | solution.py:27
  22.5 45.0 %copy-start.4 = (bf16[512,768]{1,0:T(8,128)(2,1)}, bf16[512,768]{1,0:T(8,128)(2,1)S(1)}, u32[]{:S(2)}) copy-start(bf16[512,768]{1,0:T(8,128)(2,1)S(1)} %collective-permute-done) | copy-start | bytes 2359300
  68.7 1.9 %copy-start.1 = (bf16[512,2,512]{0,2,1:T(8,128)(2,1)}, bf16[512,2,512]{0,2,1:T(8,128)(2,1)S(1)}, u32[]{:S(2)}) copy-start(bf16[512,2,512]{0,2,1:T(8,128)(2,1)S(1)} %multiply_convert_fusion) | copy-start | bytes 3145732
  70.6 4.4 %collective-permute-start.1 = (bf16[512,768]{1,0:T(8,128)(2,1)}, bf16[512,768]{1,0:T(8,128)(2,1)S(1)}, u32[]{:S(2)}, u32[]{:S(2)}) collective-permute-start(bf16[512,768]{1,0:T(8,128)(2,1)} %bitcast_convert_fusion), channel_id=1, source_target_pairs={{0,1},{1,0},{2,3},{3,2},{4,5},{5,4},{6,7},{7,6},{8,9},{9,8},{10,11... | collective-permute-start | bytes 2359304 | tf_op jit(solution)/shard_map/ppermute | solution.py:27
  73.8 1.1 copy-start.3
  111.8 12.2 %all-to-all-start.5 = ((bf16[16,8,768]{2,1,0:T(8,128)(2,1)}), bf16[16,8,768]{2,1,0:T(8,128)(2,1)S(1)}, u32[]{:S(2)}, u32[]{:S(2)}) async-start(bf16[16,8,768]{2,1,0:T(8,128)(2,1)} %broadcast_in_dim.80), calls=%async_computation.5 | async-start | bytes 393216 | tf_op jit(solution)/shard_map/all_to_all | solution.py:16
  117.3 2.4 %copy-start.2 = (bf16[512,2,512]{0,2,1:T(8,128)(2,1)S(1)}, bf16[512,2,512]{0,2,1:T(8,128)(2,1)}, u32[]{:S(2)}) copy-start(bf16[512,2,512]{0,2,1:T(8,128)(2,1)} %copy-done.1) | copy-start | bytes 3145732
  117.3 2.4 %copy-start.5 = (bf16[512,768]{1,0:T(8,128)(2,1)S(1)}, bf16[512,768]{1,0:T(8,128)(2,1)}, u32[]{:S(2)}) copy-start(bf16[512,768]{1,0:T(8,128)(2,1)} %copy-done.4) | copy-start | bytes 2359300

commit v8 on v7

--- a/solution.py
+++ b/solution.py
@@ -18,9 +18,8 @@
 
 def shared_and_scattered(x, far, near):
     tiles = x.reshape(lax.axis_size(near), -1, x.shape[-1])
-    copies = jnp.broadcast_to(tiles, (lax.axis_size(far), *tiles.shape))
-    copies = copies.reshape(-1, *tiles.shape[1:])
-    return lax.all_to_all(copies, (*far, near), split_axis=0, concat_axis=0, tiled=True)
+    copies = jnp.repeat(tiles, lax.axis_size(far), axis=0)
+    return lax.all_to_all(copies, (near, *far), split_axis=0, concat_axis=0, tiled=True)
 
 
 def other_core(x):

time: 127 us -> 127 us (level)
  blocking collectives: 94.8 us -> 92.9 us
  starting transfers between devices: 9.4 us -> 10.9 us
    all_to_all x2, blocking collectives: 45.8 us -> 44.1 us  [shared_and_scattered(): lax.all_to_all(copies, (near, *far), split_axis=0, concat_axis=0, tiled=T...]
    all_to_all x1, starting transfers between devices: 5.59 us -> 7.03 us  [copy_for_each(): return lax.all_to_all(copies, axis, split_axis=0, concat_axis=0, tiled=True)]
where the time goes in v8:
time: 127 us; the launch traced here: 125 us
  blocking collectives  92.9 us (73%)
  matrix products  11.7 us (9%)
  starting transfers between devices  10.9 us (9%)
  local copies, waits for them, and re-layouts  3.34 us (3%)
  between operations  2.72 us (2%)
  other arithmetic  2.18 us (2%)
  waiting for transfers between devices  1.68 us (1%)
    all_to_all x2, blocking collectives, shared_and_scattered(): lax.all_to_all(copies, (near, *far), split_axis=0, concat_axis=0, tiled=T...  44.1 us
    all_to_all x2, blocking collectives, copy_for_each(): return lax.all_to_all(copies, axis, split_axis=0, concat_axis=0, tiled=True)  30.7 us
    all_to_all x1, blocking collectives, sent_and_summed(): lax.all_to_all(tiles, axis, split_axis=0, concat_axis=0, tiled=True)  18 us
    all_to_all x1, starting transfers between devices, copy_for_each(): return lax.all_to_all(copies, axis, split_axis=0, concat_axis=0, tiled=True)  7.03 us
    dot_general x2, matrix products, per_device(): lax.dot_general(w, rows, (((0,), (0,)), ((), ())), preferred_element_type...  4.46 us
    dot_general x4, matrix products, scored(): lax.dot_general(rows, documents, (((1,), (2,)), ((), ())), preferred_elem...  4.29 us
    ppermute x2, starting transfers between devices, other_core(): return lax.ppermute(x, 'c', [(0, 1), (1, 0)])  3.82 us
    dot_general x2, matrix products, grad_of_rows(): lax.dot_general(weighted, documents, (((1, 2), (0, 1)), ((), ())), prefer...  2.95 us
  transfers between devices with their start and end apart: 3, of which 3 were waited for; matrix products, arithmetic and copies ran while one was open for 7% of the time, Pallas kernels for 0%

profile of v8, /device:TPU:6, one launch (start us, length us, event | category | flops | bytes accessed | tf_op | source)
XLA Modules:
  0.0 125.4 jit_solution(14956520031993856025)
XLA Ops:
  0.7 1.1 broadcast_in_dim.68
  1.8 16.6 %all_to_all.30 = bf16[4,4,32,768]{3,2,1,0:T(8,128)(2,1)S(1)} all-to-all(bf16[4,4,32,768]{3,2,1,0:T(8,128)(2,1)S(1)} %broadcast_in_dim.68), channel_id=1, replica_groups=mesh['x'=4,'h'=4,'m'=2,'p'=2,'y'=4,'c'=2] {'y'}, dimensions={0} | all-to-all | bytes 1572864 | tf_op jit(solution)/shard_map/all_to_all | solution.py:16
  18.3 1.9 %collective-permute-start = (bf16[512,768]{1,0:T(8,128)(2,1)S(1)}, bf16[512,768]{1,0:T(8,128)(2,1)S(1)}, u32[]{:S(2)}, u32[]{:S(2)}) collective-permute-start(bf16[512,768]{1,0:T(8,128)(2,1)S(1)} %bitcast.65), channel_id=1, source_target_pairs={{0,1},{1,0},{2,3},{3,2},{4,5},{5,4},{6,7},{7,6},{8,9},{9,8},{10,11... | collective-permute-start | bytes 2359304 | tf_op jit(solution)/shard_map/ppermute | solution.py:26
  20.3 0.1 reshape.129
  20.4 0.1 reshape.130
  20.5 1.0 multiply_reduce_fusion.1
  21.5 0.4 exponential_reduce_fusion.1
  21.9 0.6 collective-permute-done
  22.5 1.0 multiply_reduce_fusion
  23.5 0.4 exponential_reduce_fusion
  24.0 28.2 %all_to_all.31 = f32[16,8,128]{2,1,0:T(8,128)S(1)} all-to-all(f32[16,8,128]{2,1,0:T(8,128)S(1)} %bitcast.75), channel_id=1, replica_groups=mesh['x'=4,'h'=4,'m'=2,'p'=2,'y'=4,'c'=2] {'p','h','m'}, dimensions={0} | all-to-all | bytes 131072 | tf_op jit(solution)/shard_map/all_to_all | solution.py:22
  52.2 14.2 %all_to_all.32 = f32[64,8,128]{2,1,0:T(8,128)S(1)} all-to-all(f32[64,8,128]{2,1,0:T(8,128)S(1)} %broadcast_in_dim.70), channel_id=1, replica_groups=mesh['x'=4,'h'=4,'m'=2,'p'=2,'y'=4,'c'=2] {'y','c','x','p'}, dimensions={0} | all-to-all | bytes 524288 | tf_op jit(solution)/shard_map/all_to_all | solution.py:16
  66.5 0.1 add.55
  66.7 0.1 reduce_sum.109
  67.3 0.1 slice.36
  67.4 1.1 multiply_convert_fusion
  68.5 1.9 %bitcast_convert_fusion = bf16[512,768]{1,0:T(8,128)(2,1)} fusion(bf16[512,2,512]{0,2,1:T(8,128)(2,1)S(1)} %multiply_convert_fusion, bf16[2,512,768]{2,1,0:T(8,128)(2,1)S(1)} %copy-done), kind=kOutput, calls=%fused_computation.7 | convolution fusion | flops 805699584 | bytes 3407872 | tf_op jit(solution)/shard_map/dot_general | solution.py:103
  70.4 1.9 %collective-permute-start.1 = (bf16[512,768]{1,0:T(8,128)(2,1)}, bf16[512,768]{1,0:T(8,128)(2,1)S(1)}, u32[]{:S(2)}, u32[]{:S(2)}) collective-permute-start(bf16[512,768]{1,0:T(8,128)(2,1)} %bitcast_convert_fusion), channel_id=1, source_target_pairs={{0,1},{1,0},{2,3},{3,2},{4,5},{5,4},{6,7},{7,6},{8,9},{9,8},{10,11... | collective-permute-start | bytes 2359304 | tf_op jit(solution)/shard_map/ppermute | solution.py:26
  72.5 1.1 multiply_convert_fusion.1
  73.6 1.0 convolution_bitcast_fusion
  74.7 0.1 collective-permute-done.1
  74.8 0.2 add_convert_fusion.1
  75.0 18.0 %all_to_all.33 = bf16[32,16,768]{2,1,0:T(8,128)(2,1)S(1)} all-to-all(bf16[32,16,768]{2,1,0:T(8,128)(2,1)S(1)} %bitcast.69), channel_id=1, replica_groups=mesh['x'=4,'h'=4,'m'=2,'p'=2,'y'=4,'c'=2] {'y','x','p'}, dimensions={0} | all-to-all | bytes 1572864 | tf_op jit(solution)/shard_map/all_to_all | solution.py:36
  93.1 0.1 reduce_sum.113
  93.2 15.9 %all_to_all.34 = bf16[8,8,768]{2,1,0:T(8,128)(2,1)S(1)} all-to-all(bf16[8,8,768]{2,1,0:T(8,128)(2,1)S(1)} %bitcast.73), channel_id=1, replica_groups=mesh['x'=4,'h'=4,'m'=2,'p'=2,'y'=4,'c'=2] {'m','h'}, dimensions={0} | all-to-all | bytes 196608 | tf_op jit(solution)/shard_map/all_to_all | solution.py:22
  109.1 0.7 broadcast_in_dim.80
  109.8 7.0 %all-to-all-start.5 = ((bf16[16,8,768]{2,1,0:T(8,128)(2,1)}), bf16[16,8,768]{2,1,0:T(8,128)(2,1)S(1)}, u32[]{:S(2)}, u32[]{:S(2)}) async-start(bf16[16,8,768]{2,1,0:T(8,128)(2,1)} %broadcast_in_dim.80), calls=%async_computation.5 | async-start | bytes 393216 | tf_op jit(solution)/shard_map/all_to_all | solution.py:16
  116.9 2.3 %fusion.10 = f32[2,512,768]{2,1,0:T(8,128)S(1)} fusion(bf16[512,2,512]{0,2,1:T(8,128)(2,1)} %copy-done.3, bf16[512,768,1]{1,0,2:T(8,128)(2,1)S(1)} %bitcast.68), kind=kOutput, calls=%fused_computation.40 | convolution fusion | flops 805306368 | bytes 4980736 | tf_op jit(solution)/shard_map/dot_general | solution.py:118
  119.2 2.1 %add_convert_fusion = bf16[2,512,768]{2,1,0:T(8,128)(2,1)} fusion(f32[2,512,768]{2,1,0:T(8,128)S(1)} %fusion.10, bf16[512,2,512]{0,2,1:T(8,128)(2,1)S(1)} %copy-done.2, bf16[512,768]{1,0:T(8,128)(2,1)S(1)} %copy-done.5), kind=kOutput, calls=%fused_computation | convolution fusion | flops 806879232 | bytes 6553600 | tf_op jit(solution)/shard_map/dot_general | solution.py:118
  121.4 0.6 subtract_reduce_fusion
  122.6 0.9 all-to-all-done.5
  123.5 0.7 copy.33
  (49 shorter events, 0.9 us)
Async XLA Ops:
  0.6 19.8 %copy-start = (bf16[2,512,768]{2,1,0:T(8,128)(2,1)S(1)}, bf16[2,512,768]{2,1,0:T(8,128)(2,1)}, u32[]{:S(2)}) copy-start(bf16[2,512,768]{2,1,0:T(8,128)(2,1)} %param.4) | copy-start | bytes 4718596
  0.6 19.6 %copy-start.6 = (s32[32,4]{0,1:T(4,128)S(1)}, s32[32,4]{0,1:T(4,128)}, u32[]{:S(2)}) copy-start(s32[32,4]{0,1:T(4,128)} %param.5) | copy-start | bytes 1540
  18.3 4.2 %collective-permute-start = (bf16[512,768]{1,0:T(8,128)(2,1)S(1)}, bf16[512,768]{1,0:T(8,128)(2,1)S(1)}, u32[]{:S(2)}, u32[]{:S(2)}) collective-permute-start(bf16[512,768]{1,0:T(8,128)(2,1)S(1)} %bitcast.65), channel_id=1, source_target_pairs={{0,1},{1,0},{2,3},{3,2},{4,5},{5,4},{6,7},{7,6},{8,9},{9,8},{10,11... | collective-permute-start | bytes 2359304 | tf_op jit(solution)/shard_map/ppermute | solution.py:26
  22.5 44.8 %copy-start.4 = (bf16[512,768]{1,0:T(8,128)(2,1)}, bf16[512,768]{1,0:T(8,128)(2,1)S(1)}, u32[]{:S(2)}) copy-start(bf16[512,768]{1,0:T(8,128)(2,1)S(1)} %collective-permute-done) | copy-start | bytes 2359300
  68.5 1.9 %copy-start.1 = (bf16[512,2,512]{0,2,1:T(8,128)(2,1)}, bf16[512,2,512]{0,2,1:T(8,128)(2,1)S(1)}, u32[]{:S(2)}) copy-start(bf16[512,2,512]{0,2,1:T(8,128)(2,1)S(1)} %multiply_convert_fusion) | copy-start | bytes 3145732
  70.4 4.4 %collective-permute-start.1 = (bf16[512,768]{1,0:T(8,128)(2,1)}, bf16[512,768]{1,0:T(8,128)(2,1)S(1)}, u32[]{:S(2)}, u32[]{:S(2)}) collective-permute-start(bf16[512,768]{1,0:T(8,128)(2,1)} %bitcast_convert_fusion), channel_id=1, source_target_pairs={{0,1},{1,0},{2,3},{3,2},{4,5},{5,4},{6,7},{7,6},{8,9},{9,8},{10,11... | collective-permute-start | bytes 2359304 | tf_op jit(solution)/shard_map/ppermute | solution.py:26
  73.6 1.1 copy-start.3
  109.8 13.7 %all-to-all-start.5 = ((bf16[16,8,768]{2,1,0:T(8,128)(2,1)}), bf16[16,8,768]{2,1,0:T(8,128)(2,1)S(1)}, u32[]{:S(2)}, u32[]{:S(2)}) async-start(bf16[16,8,768]{2,1,0:T(8,128)(2,1)} %broadcast_in_dim.80), calls=%async_computation.5 | async-start | bytes 393216 | tf_op jit(solution)/shard_map/all_to_all | solution.py:16
  116.9 2.4 %copy-start.2 = (bf16[512,2,512]{0,2,1:T(8,128)(2,1)S(1)}, bf16[512,2,512]{0,2,1:T(8,128)(2,1)}, u32[]{:S(2)}) copy-start(bf16[512,2,512]{0,2,1:T(8,128)(2,1)} %copy-done.1) | copy-start | bytes 3145732
  116.9 2.4 %copy-start.5 = (bf16[512,768]{1,0:T(8,128)(2,1)S(1)}, bf16[512,768]{1,0:T(8,128)(2,1)}, u32[]{:S(2)}) copy-start(bf16[512,768]{1,0:T(8,128)(2,1)} %copy-done.4) | copy-start | bytes 2359300
